TPU v7x, 32 devices: a whole 2x2x4 slice. The times are simulated.
32 devices in a mesh: team: 2 (over x), blk: 4 (over z), head: 4 (over y, core).
Axes of the slice: x: 2, y: 2, z: 4, core: 2. Of those that a mesh axis runs over, the one named last changes fastest.
Arguments:
- queries: bfloat16 [1024, 8, 8, 128], P('blk', 'head', 'team'), may hold values from -40 to 40
- features: bfloat16 [1024, 8192], P('blk', ('team', 'head')), may hold values from -6 to 6
- adapter_down: bfloat16 [4, 8192, 64], P(None, ('team', 'head')), may hold values from -0.0625 to 0.0625
- adapter_key_up: bfloat16 [4, 64, 8, 128], P(None, None, 'head'), may hold values from -0.75 to 0.75
- adapter_value_up: bfloat16 [4, 64, 8, 128], P(None, None, 'head'), may hold values from -0.75 to 0.75
- base_key: bfloat16 [1024, 8, 128], P('blk', 'head'), may hold values from -6 to 6
- base_value: bfloat16 [1024, 8, 128], P('blk', 'head'), may hold values from -24 to 24
- prefix_key: bfloat16 [2048, 8, 128], P('blk', 'head'), may hold values from -7 to 7
- prefix_value: bfloat16 [2048, 8, 128], P('blk', 'head'), may hold values from -24 to 24
- adapter_ids: int32 [4], replicated, may hold values from 0 to 3
- block_order: int32 [4], replicated, may hold values from 0 to 15
Outputs:
- attended: bfloat16 [1024, 8, 8, 128], P('blk', 'head', 'team')
All inputs are finite; a program needn't handle non-finite values.
Results may differ from a plain program's by a relative error of at most 0.011.
Values may be sent and summed in bfloat16 or wider, within the bound.
No kernel may reach another device: no remote copies, remote signals or barrier semaphores. Data moves between devices by JAX's collectives and lax.ppermute only.
A program may use at most 64 MiB of HBM per device.

v0:
```python
import functools
import math

import jax
import jax.numpy as jnp
from jax import lax
from jax.experimental import pallas as pl
from jax.experimental.pallas import tpu as pltpu
from jax.sharding import PartitionSpec as P


NEG_FILL = -1e30
LOG2E = 1.4426950408889634
TILE = 128
UNROLL = 8
LIMIT = 20 * 2**20
VMEM = pl.BlockSpec(memory_space=pltpu.VMEM)
SMEM = pl.BlockSpec(memory_space=pltpu.SMEM)


def dot_t(a, b):
    return lax.dot_general(a, b, (((1,), (1,)), ((), ())), preferred_element_type=jnp.float32)


def latent_kernel(ids_ref, order_ref, features_ref, down_ref, out_ref, bound_ref, held, sem):
    me = lax.axis_index("blk")
    copy = pltpu.make_async_copy(down_ref.at[ids_ref[me]], held, sem)
    copy.start()
    tokens = features_ref.shape[0]
    for mask in range(order_ref.shape[0]):
        bound = (order_ref[me] - order_ref[me ^ mask]) * tokens
        bound_ref[mask : mask + 1, :] = jnp.full((1, bound_ref.shape[1]), bound, jnp.int32)
    copy.wait()
    out_ref[...] = dot_t(held[...], features_ref[...])


def partial_latent(ids, order, features, down):
    tokens, depth = features.shape
    rank = down.shape[1]
    return pl.pallas_call(
        latent_kernel,
        out_shape=[
            jax.ShapeDtypeStruct((rank, tokens), jnp.float32),
            jax.ShapeDtypeStruct((order.shape[0], 128), jnp.int32),
        ],
        in_specs=[SMEM, SMEM, VMEM, pl.BlockSpec(memory_space=pl.ANY)],
        out_specs=[VMEM, VMEM],
        scratch_shapes=[pltpu.VMEM((rank, depth), down.dtype), pltpu.SemaphoreType.DMA(())],
        compiler_params=pltpu.CompilerParams(vmem_limit_bytes=LIMIT),
        cost_estimate=pl.CostEstimate(
            flops=2 * tokens * depth * rank,
            bytes_accessed=2 * depth * (tokens + rank),
            transcendentals=0,
        ),
        name="partial_latent",
    )(ids, order, features, down)


def expand_kernel(ids_ref, first, second, key_up, value_up, key_base, value_base, out_ref):
    chosen = ids_ref[lax.axis_index("blk")]
    latent = (first[...] + second[...]).astype(jnp.bfloat16)
    tokens = key_base.shape[0]
    for n, (up, base) in enumerate(((key_up, key_base), (value_up, value_base))):
        delta = lax.dot_general(
            latent, up[chosen], (((0,), (0,)), ((), ())), preferred_element_type=jnp.float32
        )
        out_ref[n * tokens : (n + 1) * tokens, :] = (
            base[...].astype(jnp.float32) + delta
        ).astype(jnp.bfloat16)


def expand(ids, first, second, key_up, value_up, key_base, value_base):
    tokens, head_dim = key_base.shape
    return pl.pallas_call(
        expand_kernel,
        out_shape=jax.ShapeDtypeStruct((2 * tokens, head_dim), jnp.bfloat16),
        in_specs=[SMEM] + [VMEM] * 6,
        out_specs=VMEM,
        compiler_params=pltpu.CompilerParams(vmem_limit_bytes=LIMIT),
        cost_estimate=pl.CostEstimate(
            flops=4 * tokens * head_dim * first.shape[0],
            bytes_accessed=8 * tokens * head_dim,
            transcendentals=0,
        ),
        name="expand",
    )(ids, first, second, key_up, value_up, key_base, value_base)


def wide(value, width):
    return jnp.concatenate([value] * (width // value.shape[1]), axis=1)


def attend_kernel(span, masks, carried, final, group, scale, *refs):
    bound_ref, refs = (None, refs) if set(masks) == {None} else (refs[0], refs[1:])
    q_ref, refs = refs[0], refs[1:]
    state_refs, refs = refs[: 2 * carried], refs[2 * carried :]
    kv_refs, outs = refs[: len(masks)], refs[len(masks) :]
    head_dim = q_ref.shape[1]
    start, rows = span

    def body(i, _):
        here = pl.ds(pl.multiple_of(i * TILE, TILE), TILE)
        at = pl.ds(pl.multiple_of(start + i * TILE, TILE), TILE)
        q = q_ref[at, :]
        scores = []
        top = None
        for kv, mask in zip(kv_refs, masks):
            half = kv.shape[0] // 2
            s = dot_t(q, kv[:half, :])
            if mask is not None:
                limit = bound_ref[mask : mask + 1, :] * group + (start + i * TILE)
                ahead = lax.broadcasted_iota(jnp.int32, (TILE, half), 1) * group
                ahead = ahead - lax.broadcasted_iota(jnp.int32, (TILE, half), 0)
                s = jnp.where(ahead <= wide(limit, half), s, NEG_FILL)
            scores.append(s)
            most = jnp.max(s, axis=1, keepdims=True)
            top = most if top is None else jnp.maximum(top, most)
        top = jnp.broadcast_to(top * scale, (TILE, head_dim))
        acc = None
        if carried:
            old = state_refs[0][at, :]
            top = jnp.maximum(top, old)
            acc = state_refs[1][at, :] * wide(jnp.exp2(old - top), 2 * head_dim)
        for s, kv in zip(scores, kv_refs):
            half = kv.shape[0] // 2
            p = jnp.exp2(s * scale - wide(top, half))
            values = kv[half:, :]
            values = jnp.concatenate([values, jnp.ones_like(values)], axis=1)
            part = jnp.dot(p.astype(jnp.bfloat16), values, preferred_element_type=jnp.float32)
            acc = part if acc is None else acc + part
        if final:
            outs[0][here, :] = (acc[:, :head_dim] / acc[:, head_dim:]).astype(jnp.bfloat16)
        else:
            outs[0][here, :] = top
            outs[1][here, :] = acc
        return 0

    lax.fori_loop(0, rows // TILE, body, 0, unroll=min(UNROLL, rows // TILE))


def attend(bounds, queries, state, pieces, final, group, scale, span=None):
    span = span or (0, queries.shape[0])
    rows, head_dim = span[1], queries.shape[1]
    masks = tuple(mask for mask, _ in pieces)
    keys = sum(piece.shape[0] // 2 for _, piece in pieces)
    if final:
        shapes = [jax.ShapeDtypeStruct((rows, head_dim), jnp.bfloat16)]
    else:
        shapes = [
            jax.ShapeDtypeStruct((rows, head_dim), jnp.float32),
            jax.ShapeDtypeStruct((rows, 2 * head_dim), jnp.float32),
        ]
    operands = [queries, *(state or []), *(piece for _, piece in pieces)]
    table = [] if set(masks) == {None} else [bounds]
    return pl.pallas_call(
        functools.partial(attend_kernel, span, masks, state is not None, final, group, scale),
        out_shape=shapes,
        in_specs=[VMEM] * len(table + operands),
        out_specs=[VMEM] * len(shapes),
        compiler_params=pltpu.CompilerParams(vmem_limit_bytes=LIMIT),
        cost_estimate=pl.CostEstimate(
            flops=6 * rows * keys * head_dim,
            bytes_accessed=rows * head_dim * 4,
            transcendentals=rows * keys,
        ),
        name="attend",
    )(*table, *operands)


def butterfly(value, axis, size):
    step = 1
    pair = (value, None)
    while step < size:
        value = pair[0] if pair[1] is None else pair[0] + pair[1]
        pair = (value, lax.ppermute(value, axis, [(i, i ^ step) for i in range(size)]))
        step *= 2
    return pair


def gather_blocks(value, count, before=None):
    held = {0: value}
    step = count // 2
    while step:
        perm = [(i, i ^ step) for i in range(count)]
        for mask in list(held):
            sent = held[mask]
            if before is not None and (mask ^ step) == count - 1:
                sent, before = lax.optimization_barrier((sent, before))
            held[mask ^ step] = lax.ppermute(sent, "blk", perm)
        step //= 2
    return held, before


def on_device(
    queries,
    features,
    adapter_down,
    adapter_key_up,
    adapter_value_up,
    base_key,
    base_value,
    prefix_key,
    prefix_value,
    adapter_ids,
    block_order,
):
    block_count = lax.axis_size("blk")
    team_count = lax.axis_size("team")
    query_dev, _, group_dev, head_dim = queries.shape
    mine = lax.axis_index("team") & 1
    scale = LOG2E / math.sqrt(head_dim)
    rows = query_dev * group_dev

    def swap(value):
        return lax.ppermute(value, "team", [(i, i ^ 1) for i in range(team_count)])

    def pick(array, axis, other=False):
        index = 1 - mine if other else mine
        return lax.dynamic_index_in_dim(array, index, axis, keepdims=False)

    latent, bounds = partial_latent(adapter_ids, block_order, features, jnp.swapaxes(adapter_down, 1, 2))
    own_prefix = pick(jnp.concatenate([prefix_key, prefix_value], axis=0), 1)
    first, second = butterfly(latent, "head", lax.axis_size("head"))
    first, second = butterfly(first + second, "team", team_count)

    prefix, _ = gather_blocks(own_prefix, block_count)
    own_queries = pick(queries, 1).reshape(rows, head_dim)
    far_queries = swap(pick(queries, 1, True).reshape(rows, head_dim))
    own_new = expand(
        adapter_ids,
        first,
        second,
        pick(adapter_key_up, 2),
        pick(adapter_value_up, 2),
        pick(base_key, 1),
        pick(base_value, 1),
    )
    last = block_count - 1
    early = [(None, piece) for mask, piece in prefix.items() if mask != last]
    own_state = attend(bounds, own_queries, None, early, False, group_dev, scale)
    new, own_state = gather_blocks(own_new, block_count, own_state)
    far_state = attend(bounds, far_queries, None, early, False, group_dev, scale)
    middle = [(mask, new[mask]) for mask in new if mask in (0, block_count // 2)]
    tail = [(None, prefix[last])]
    tail += [(mask, new[mask]) for mask in new if mask not in (0, block_count // 2)]
    far_state = attend(bounds, far_queries, far_state, middle, False, group_dev, scale)
    own_state = attend(bounds, own_queries, own_state, middle, False, group_dev, scale)
    far_state, own_state = lax.optimization_barrier((far_state, own_state))
    parts = 2 if rows % (2 * TILE) == 0 else 1
    part = rows // parts
    received = []
    for n in range(parts):
        span = (n * part, part)
        out = attend(bounds, far_queries, far_state, tail, True, group_dev, scale, span)[0]
        received.append(swap(out))
    own_out = attend(bounds, own_queries, own_state, tail, True, group_dev, scale)[0]
    shape = (query_dev, 1, group_dev, head_dim)
    head = lax.broadcasted_iota(jnp.int32, queries.shape, 1)
    received = jnp.concatenate(received, axis=0)
    return jnp.where(head == mine, own_out.reshape(shape), received.reshape(shape))


def solution(mesh):
    placed = (
        P("blk", "head", "team", None),
        P("blk", ("team", "head")),
        P(None, ("team", "head"), None),
        P(None, None, "head", None),
        P(None, None, "head", None),
        P("blk", "head", None),
        P("blk", "head", None),
        P("blk", "head", None),
        P("blk", "head", None),
        P(),
        P(),
    )

    return jax.shard_map(
        on_device,
        mesh=mesh,
        in_specs=placed,
        out_specs=P("blk", "head", "team", None),
        check_vma=False,
    )
```

profile of v0, /device:TPU:0, one launch (start us, length us, event | category | flops | bytes accessed | tf_op | source)
XLA Modules:
  0.0 45.6 jit_solution(7955199521377375831)
XLA Ops:
  0.0 1.0 %copy.12 = bf16[512,2,128]{2,0,1:T(8,128)(2,1)S(1)} copy(bf16[512,2,128]{2,1,0:T(2,128)(2,1)} %param.18) | data formatting | bytes 524288 | tf_op args[7]
  1.0 0.0 copy-start.1
  1.1 0.0 copy-start
  1.1 0.0 copy-start.2
  1.2 0.0 copy-start.3
  1.2 4.1 %collective-permute-start.1 = (bf16[1024,128]{1,0:T(8,128)(2,1)S(1)}, bf16[1024,128]{1,0:T(8,128)(2,1)S(1)}, u32[]{:S(2)}, u32[]{:S(2)}) collective-permute-start(bf16[1024,128]{1,0:T(8,128)(2,1)S(1)} %fusion.1.refs_1_), channel_id=1, source_target_pairs={{0,8},{4,12},{8,0},{12,4},{1,9},{5,13},{9,1},{13,5},{2,10},{6,14},... | collective-permute-start | bytes 786440 | tf_op jit(solution)/shard_map/ppermute | solution.py:189
  5.3 1.6 %collective-permute-start.2 = (bf16[1024,128]{1,0:T(8,128)(2,1)S(1)}, bf16[1024,128]{1,0:T(8,128)(2,1)S(1)}, u32[]{:S(2)}, u32[]{:S(2)}) collective-permute-start(bf16[1024,128]{1,0:T(8,128)(2,1)S(1)} %fusion.1.refs_1_), channel_id=1, source_target_pairs={{0,4},{4,0},{8,12},{12,8},{1,5},{5,1},{9,13},{13,9},{2,6},{6,2},{1... | collective-permute-start | bytes 786440 | tf_op jit(solution)/shard_map/ppermute | solution.py:189
  6.9 0.0 copy-done.3
  6.9 0.0 copy-start.4
  6.9 1.0 %partial_latent.1 = (f32[64,256]{1,0:T(8,128)S(1)}, s32[4,128]{1,0:T(4,128)S(1)}) custom-call(s32[4]{0:T(128)S(1)} %copy-done.2, s32[4]{0:T(128)S(1)} %copy-done.3, bf16[256,1024]{1,0:T(8,128)(2,1)S(1)} %copy-done, bf16[4,64,1024]{2,1,0:T(8,128)(2,1)S(1)} %bitcast.22), custom_call_target="tpu_custom_call" | custom-call | flops 33554432 | bytes 655360 | tf_op jit(solution)/shard_map/partial_latent/pallas_call | solution.py:40
  7.9 0.1 collective-permute-start.3
  8.0 0.0 copy-start.7
  8.0 0.2 constant_dynamic-slice_fusion.5
  8.2 0.0 copy-start.6
  8.3 1.6 %collective-permute-start = (bf16[1024,128]{1,0:T(8,128)(2,1)S(1)}, bf16[1024,128]{1,0:T(8,128)(2,1)S(1)}, u32[]{:S(2)}, u32[]{:S(2)}) collective-permute-start(bf16[1024,128]{1,0:T(8,128)(2,1)S(1)} %bitcast.29), channel_id=1, source_target_pairs={{0,16},{16,0},{1,17},{17,1},{2,18},{18,2},{3,19},{19,3},{4,20},{20... | collective-permute-start | bytes 786440 | tf_op jit(solution)/shard_map/ppermute | solution.py:215
  9.8 0.0 collective-permute-done.3
  9.8 1.6 %collective-permute-start.4 = (f32[64,256]{1,0:T(8,128)S(1)}, f32[64,256]{1,0:T(8,128)S(1)}, u32[]{:S(2)}, u32[]{:S(2)}) collective-permute-start(f32[64,256]{1,0:T(8,128)S(1)} %add.24), channel_id=1, source_target_pairs={{0,2},{1,3},{2,0},{3,1},{4,6},{5,7},{6,4},{7,5},{8,10},{9,11},{10,... | collective-permute-start | bytes 196616 | tf_op jit(solution)/shard_map/ppermute | solution.py:175
  11.4 0.3 constant_dynamic-slice_fusion
  11.7 0.0 copy-start.9
  11.7 0.0 copy-start.8
  11.8 2.4 %collective-permute-done.4 = f32[64,256]{1,0:T(8,128)S(1)} collective-permute-done((f32[64,256]{1,0:T(8,128)S(1)}, f32[64,256]{1,0:T(8,128)S(1)}, u32[]{:S(2)}, u32[]{:S(2)}) %collective-permute-start.4) | collective-permute-done | bytes 65568 | tf_op jit(solution)/shard_map/ppermute | solution.py:175
  14.2 1.0 %collective-permute-start.5 = (f32[64,256]{1,0:T(8,128)S(1)}, f32[64,256]{1,0:T(8,128)S(1)}, u32[]{:S(2)}, u32[]{:S(2)}) collective-permute-start(f32[64,256]{1,0:T(8,128)S(1)} %add.25.first), channel_id=1, source_target_pairs={{0,16},{16,0},{1,17},{17,1},{2,18},{18,2},{3,19},{19,3},{4,20},{20... | collective-permute-start | bytes 196616 | tf_op jit(solution)/shard_map/ppermute | solution.py:175
  15.2 0.3 constant_dynamic-slice_fusion.2
  15.5 3.0 %collective-permute-done.5.second = f32[64,256]{1,0:T(8,128)S(1)} collective-permute-done((f32[64,256]{1,0:T(8,128)S(1)}, f32[64,256]{1,0:T(8,128)S(1)}, u32[]{:S(2)}, u32[]{:S(2)}) %collective-permute-start.5) | collective-permute-done | bytes 65568 | tf_op jit(solution)/shard_map/ppermute | solution.py:175
  18.5 0.8 %expand.1.refs_4_ = bf16[512,128]{1,0:T(8,128)(2,1)S(1)} custom-call(s32[4]{0:T(128)S(1)} %copy-done.2, f32[64,256]{1,0:T(8,128)S(1)} %add.25.first, f32[64,256]{1,0:T(8,128)S(1)} %collective-permute-done.5.second, bf16[4,64,128]{2,1,0:T(8,128)(2,1)S(1)} %bitcast.26, bf16[4,64,128]{2,1,0:T(8,128)(2,1)S(1)} %bitcast.25, bf16[256,128]{1,0:T(8,128)(2,1)S(1)} %bitcast.24, ...), custom_call_target="tpu_custom_call" | custom-call | flops 8388608 | bytes 262144 | tf_op jit(solution)/shard_map/expand/pallas_call | solution.py:74
  19.3 0.4 collective-permute-start.6
  19.7 0.7 %collective-permute-start.8 = (bf16[512,128]{1,0:T(8,128)(2,1)S(1)}, bf16[512,128]{1,0:T(8,128)(2,1)S(1)}, u32[]{:S(2)}, u32[]{:S(2)}) collective-permute-start(bf16[512,128]{1,0:T(8,128)(2,1)S(1)} %expand.1.refs_4_), channel_id=1, source_target_pairs={{0,4},{4,0},{8,12},{12,8},{1,5},{5,1},{9,13},{13,9},{2,6},{6,2},{1... | collective-permute-start | bytes 393224 | tf_op jit(solution)/shard_map/ppermute | solution.py:189
  20.3 0.0 collective-permute-done.1.refs_2_
  20.3 1.4 %collective-permute-start.7 = (bf16[1024,128]{1,0:T(8,128)(2,1)S(1)}, bf16[1024,128]{1,0:T(8,128)(2,1)S(1)}, u32[]{:S(2)}, u32[]{:S(2)}) collective-permute-start(bf16[1024,128]{1,0:T(8,128)(2,1)S(1)} %collective-permute-done.1.refs_2_), channel_id=1, source_target_pairs={{0,4},{4,0},{8,12},{12,8},{1,5},{5,1},{9,13},{13,9},{2,6},{6,2},{1... | collective-permute-start | bytes 786440 | tf_op jit(solution)/shard_map/ppermute | solution.py:189
  21.7 0.0 collective-permute-done.2.refs_3_
  21.7 2.5 %attend.9 = (f32[1024,128]{1,0:T(8,128)S(1)}, f32[1024,256]{1,0:T(8,128)S(1)}) custom-call(bf16[1024,128]{1,0:T(8,128)(2,1)S(1)} %bitcast.19, bf16[1024,128]{1,0:T(8,128)(2,1)S(1)} %fusion.1.refs_1_, bf16[1024,128]{1,0:T(8,128)(2,1)S(1)} %collective-permute-done.1.refs_2_, bf16[1024,128]{1,0:T(8,128)(2,1)S(1)} %collective-permute-done.2.refs_3_), custom_call_target="tpu_custom_call" | custom-call | flops 1207959552 | bytes 524288 | tf_op jit(solution)/shard_map/attend/pallas_call | solution.py:155
  24.2 3.4 %collective-permute-done.6.refs_5_ = bf16[512,128]{1,0:T(8,128)(2,1)S(1)} collective-permute-done((bf16[512,128]{1,0:T(8,128)(2,1)S(1)}, bf16[512,128]{1,0:T(8,128)(2,1)S(1)}, u32[]{:S(2)}, u32[]{:S(2)}) %collective-permute-start.6) | collective-permute-done | bytes 131104 | tf_op jit(solution)/shard_map/ppermute | solution.py:189
  27.6 0.0 collective-permute-start.9
  27.6 0.0 collective-permute-done.refs_0_.refs_1_
  27.6 2.5 %attend.7 = (f32[1024,128]{1,0:T(8,128)S(1)}, f32[1024,256]{1,0:T(8,128)S(1)}) custom-call(bf16[1024,128]{1,0:T(8,128)(2,1)S(1)} %collective-permute-done.refs_0_.refs_1_, bf16[1024,128]{1,0:T(8,128)(2,1)S(1)} %fusion.1.refs_1_, bf16[1024,128]{1,0:T(8,128)(2,1)S(1)} %collective-permute-done.1.refs_2_, bf16[1024,128]{1,0:T(8,128)(2,1)S(1)} %collective-permute-done.2.refs_3_), custom_call_target="tpu_custom_call" | custom-call | flops 1207959552 | bytes 524288 | tf_op jit(solution)/shard_map/attend/pallas_call | solution.py:155
  30.1 1.1 %attend.10 = (f32[1024,128]{1,0:T(8,128)S(1)}, f32[1024,256]{1,0:T(8,128)S(1)}) custom-call(s32[4,128]{1,0:T(4,128)S(1)} %get-tuple-element.22.refs_0_, bf16[1024,128]{1,0:T(8,128)(2,1)S(1)} %bitcast.20, f32[1024,128]{1,0:T(8,128)S(1)} %get-tuple-element.30.refs_2_, f32[1024,256]{1,0:T(8,128)S(1)} %get-tuple-element.31.refs_3_, ...), custom_call_target="tpu_custom_call" | custom-call | flops 402653184 | bytes 524288 | tf_op jit(solution)/shard_map/attend/pallas_call | solution.py:155
  31.2 1.1 %attend.8 = (f32[1024,128]{1,0:T(8,128)S(1)}, f32[1024,256]{1,0:T(8,128)S(1)}) custom-call(s32[4,128]{1,0:T(4,128)S(1)} %get-tuple-element.22.refs_0_, bf16[1024,128]{1,0:T(8,128)(2,1)S(1)} %collective-permute-done.refs_0_.refs_1_, f32[1024,128]{1,0:T(8,128)S(1)} %get-tuple-element.23.refs_2_, f32[1024,256]{1,0:T(8,128)S(1)} %get-tuple-element.24.refs_3_, ...), custom_call_target="tpu_custom_call" | custom-call | flops 402653184 | bytes 524288 | tf_op jit(solution)/shard_map/attend/pallas_call | solution.py:155
  32.3 0.0 collective-permute-done.8.refs_5_
  32.3 3.0 %collective-permute-done.9.refs_6_ = bf16[512,128]{1,0:T(8,128)(2,1)S(1)} collective-permute-done((bf16[512,128]{1,0:T(8,128)(2,1)S(1)}, bf16[512,128]{1,0:T(8,128)(2,1)S(1)}, u32[]{:S(2)}, u32[]{:S(2)}) %collective-permute-start.9) | collective-permute-done | bytes 131104 | tf_op jit(solution)/shard_map/ppermute | solution.py:189
  35.3 0.0 collective-permute-done.7.refs_4_
  35.3 1.1 %attend.12 = bf16[512,128]{1,0:T(8,128)(2,1)S(1)} custom-call(s32[4,128]{1,0:T(4,128)S(1)} %get-tuple-element.22.refs_0_, bf16[1024,128]{1,0:T(8,128)(2,1)S(1)} %collective-permute-done.refs_0_.refs_1_, f32[1024,128]{1,0:T(8,128)S(1)} %get-tuple-element.37.refs_2_, f32[1024,256]{1,0:T(8,128)S(1)} %get-tuple-element.38.refs_3_, ...), custom_call_target="tpu_custom_call" | custom-call | flops 402653184 | bytes 262144 | tf_op jit(solution)/shard_map/attend/pallas_call | solution.py:155
  36.5 1.8 %collective-permute-start.10 = (bf16[512,128]{1,0:T(8,128)(2,1)S(1)}, bf16[512,128]{1,0:T(8,128)(2,1)S(1)}, u32[]{:S(2)}, u32[]{:S(2)}) collective-permute-start(bf16[512,128]{1,0:T(8,128)(2,1)S(1)} %attend.12), channel_id=1, source_target_pairs={{0,16},{16,0},{1,17},{17,1},{2,18},{18,2},{3,19},{19,3},{4,20},{20... | collective-permute-start | bytes 393224 | tf_op jit(solution)/shard_map/ppermute | solution.py:215
  38.2 1.1 %attend.13 = bf16[512,128]{1,0:T(8,128)(2,1)S(1)} custom-call(s32[4,128]{1,0:T(4,128)S(1)} %get-tuple-element.22.refs_0_, bf16[1024,128]{1,0:T(8,128)(2,1)S(1)} %collective-permute-done.refs_0_.refs_1_, f32[1024,128]{1,0:T(8,128)S(1)} %get-tuple-element.37.refs_2_, f32[1024,256]{1,0:T(8,128)S(1)} %get-tuple-element.38.refs_3_, ...), custom_call_target="tpu_custom_call" | custom-call | flops 402653184 | bytes 262144 | tf_op jit(solution)/shard_map/attend/pallas_call | solution.py:155
  39.4 0.4 collective-permute-start.11
  39.8 1.8 %attend.11 = bf16[1024,128]{1,0:T(8,128)(2,1)S(1)} custom-call(s32[4,128]{1,0:T(4,128)S(1)} %get-tuple-element.22.refs_0_, bf16[1024,128]{1,0:T(8,128)(2,1)S(1)} %bitcast.21, f32[1024,128]{1,0:T(8,128)S(1)} %get-tuple-element.34.refs_2_, f32[1024,256]{1,0:T(8,128)S(1)} %get-tuple-element.35.refs_3_, bf16[1024,128]{1,0:T(8,128)(2,1)S(1)} %collective-permute-done.7.refs_4_, ...), custom_call_target="tpu_custom_call" | custom-call | flops 805306368 | bytes 524288 | tf_op jit(solution)/shard_map/attend/pallas_call | solution.py:155
  41.6 1.1 %collective-permute-done.10 = bf16[512,128]{1,0:T(8,128)(2,1)S(1)} collective-permute-done((bf16[512,128]{1,0:T(8,128)(2,1)S(1)}, bf16[512,128]{1,0:T(8,128)(2,1)S(1)}, u32[]{:S(2)}, u32[]{:S(2)}) %collective-permute-start.10) | collective-permute-done | bytes 131104 | tf_op jit(solution)/shard_map/ppermute | solution.py:215
  42.7 1.7 %collective-permute-done.11 = bf16[512,128]{1,0:T(8,128)(2,1)S(1)} collective-permute-done((bf16[512,128]{1,0:T(8,128)(2,1)S(1)}, bf16[512,128]{1,0:T(8,128)(2,1)S(1)}, u32[]{:S(2)}, u32[]{:S(2)}) %collective-permute-start.11) | collective-permute-done | bytes 131104 | tf_op jit(solution)/shard_map/ppermute | solution.py:215
  44.4 1.1 %broadcast_select_fusion = bf16[256,2,4,128]{3,2,1,0:T(4,128)(2,1)} fusion(pred[2]{0:T(512)(128)(4,1)S(1)} %iota_compare_fusion, bf16[256,4,128]{2,1,0:T(4,128)(2,1)S(1)} %bitcast.28, bf16[256,4,128]{2,1,0:T(4,128)(2,1)S(1)} %bitcast.27), kind=kLoop, calls=%fused_computation.2 | loop fusion | flops 262144 | bytes 1048578 | tf_op jit(solution)/shard_map/jit(_where)/select_n | solution.py:260
  (20 shorter events, 0.2 us)
Async XLA Ops:
  0.0 1.0 %copy-start.5 = (bf16[512,2,128]{2,1,0:T(2,128)(2,1)S(1)}, bf16[512,2,128]{2,1,0:T(2,128)(2,1)}, u32[]{:S(2)}) copy-start(bf16[512,2,128]{2,1,0:T(2,128)(2,1)} %param.19) | copy-start | bytes 786436
  1.0 5.8 %copy-start.1 = (bf16[4,1024,64]{1,2,0:T(8,128)(2,1)S(1)}, bf16[4,1024,64]{1,2,0:T(8,128)(2,1)}, u32[]{:S(2)}) copy-start(bf16[4,1024,64]{1,2,0:T(8,128)(2,1)} %param.13) | copy-start | bytes 1572868
  1.1 5.8 %copy-start = (bf16[256,1024]{1,0:T(8,128)(2,1)S(1)}, bf16[256,1024]{1,0:T(8,128)(2,1)}, u32[]{:S(2)}) copy-start(bf16[256,1024]{1,0:T(8,128)(2,1)} %features_ref.1) | copy-start | bytes 1572868
  1.1 5.7 %copy-start.2 = (s32[4]{0:T(128)S(1)}, s32[4]{0:T(128)}, u32[]{:S(2)}) copy-start(s32[4]{0:T(128)} %ids_ref.3) | copy-start | bytes 52
  1.2 5.7 %copy-start.3 = (s32[4]{0:T(128)S(1)}, s32[4]{0:T(128)}, u32[]{:S(2)}) copy-start(s32[4]{0:T(128)} %order_ref.1) | copy-start | bytes 52
  1.2 19.2 %collective-permute-start.1 = (bf16[1024,128]{1,0:T(8,128)(2,1)S(1)}, bf16[1024,128]{1,0:T(8,128)(2,1)S(1)}, u32[]{:S(2)}, u32[]{:S(2)}) collective-permute-start(bf16[1024,128]{1,0:T(8,128)(2,1)S(1)} %fusion.1.refs_1_), channel_id=1, source_target_pairs={{0,8},{4,12},{8,0},{12,4},{1,9},{5,13},{9,1},{13,5},{2,10},{6,14},... | collective-permute-start | bytes 786440 | tf_op jit(solution)/shard_map/ppermute | solution.py:189
  5.3 16.4 %collective-permute-start.2 = (bf16[1024,128]{1,0:T(8,128)(2,1)S(1)}, bf16[1024,128]{1,0:T(8,128)(2,1)S(1)}, u32[]{:S(2)}, u32[]{:S(2)}) collective-permute-start(bf16[1024,128]{1,0:T(8,128)(2,1)S(1)} %fusion.1.refs_1_), channel_id=1, source_target_pairs={{0,4},{4,0},{8,12},{12,8},{1,5},{5,1},{9,13},{13,9},{2,6},{6,2},{1... | collective-permute-start | bytes 786440 | tf_op jit(solution)/shard_map/ppermute | solution.py:189
  6.9 1.1 %copy-start.4 = (bf16[256,2,4,128]{3,2,1,0:T(4,128)(2,1)S(1)}, bf16[256,2,4,128]{3,2,1,0:T(4,128)(2,1)}, u32[]{:S(2)}) copy-start(bf16[256,2,4,128]{3,2,1,0:T(4,128)(2,1)} %param.11) | copy-start | bytes 1572868
  7.9 1.9 %collective-permute-start.3 = (f32[64,256]{1,0:T(8,128)S(1)}, f32[64,256]{1,0:T(8,128)S(1)}, u32[]{:S(2)}, u32[]{:S(2)}) collective-permute-start(f32[64,256]{1,0:T(8,128)S(1)} %get-tuple-element.25), channel_id=1, source_target_pairs={{0,1},{1,0},{2,3},{3,2},{4,5},{5,4},{6,7},{7,6},{8,9},{9,8},{10,11... | collective-permute-start | bytes 196616 | tf_op jit(solution)/shard_map/ppermute | solution.py:175
  8.0 3.4 %copy-start.7 = (bf16[256,2,128]{2,1,0:T(2,128)(2,1)S(1)}, bf16[256,2,128]{2,1,0:T(2,128)(2,1)}, u32[]{:S(2)}) copy-start(bf16[256,2,128]{2,1,0:T(2,128)(2,1)} %param.16) | copy-start | bytes 393220
  8.2 3.2 %copy-start.6 = (bf16[256,2,128]{2,1,0:T(2,128)(2,1)S(1)}, bf16[256,2,128]{2,1,0:T(2,128)(2,1)}, u32[]{:S(2)}) copy-start(bf16[256,2,128]{2,1,0:T(2,128)(2,1)} %param.17) | copy-start | bytes 393220
  8.3 19.3 %collective-permute-start = (bf16[1024,128]{1,0:T(8,128)(2,1)S(1)}, bf16[1024,128]{1,0:T(8,128)(2,1)S(1)}, u32[]{:S(2)}, u32[]{:S(2)}) collective-permute-start(bf16[1024,128]{1,0:T(8,128)(2,1)S(1)} %bitcast.29), channel_id=1, source_target_pairs={{0,16},{16,0},{1,17},{17,1},{2,18},{18,2},{3,19},{19,3},{4,20},{20... | collective-permute-start | bytes 786440 | tf_op jit(solution)/shard_map/ppermute | solution.py:215
  9.8 4.3 %collective-permute-start.4 = (f32[64,256]{1,0:T(8,128)S(1)}, f32[64,256]{1,0:T(8,128)S(1)}, u32[]{:S(2)}, u32[]{:S(2)}) collective-permute-start(f32[64,256]{1,0:T(8,128)S(1)} %add.24), channel_id=1, source_target_pairs={{0,2},{1,3},{2,0},{3,1},{4,6},{5,7},{6,4},{7,5},{8,10},{9,11},{10,... | collective-permute-start | bytes 196616 | tf_op jit(solution)/shard_map/ppermute | solution.py:175
  11.7 3.5 %copy-start.9 = (bf16[4,64,2,128]{3,2,1,0:T(2,128)(2,1)S(1)}, bf16[4,64,2,128]{3,2,1,0:T(2,128)(2,1)}, u32[]{:S(2)}) copy-start(bf16[4,64,2,128]{3,2,1,0:T(2,128)(2,1)} %param.14) | copy-start | bytes 393220
  11.7 3.4 %copy-start.8 = (bf16[4,64,2,128]{3,2,1,0:T(2,128)(2,1)S(1)}, bf16[4,64,2,128]{3,2,1,0:T(2,128)(2,1)}, u32[]{:S(2)}) copy-start(bf16[4,64,2,128]{3,2,1,0:T(2,128)(2,1)} %param.15) | copy-start | bytes 393220
  14.2 4.3 %collective-permute-start.5 = (f32[64,256]{1,0:T(8,128)S(1)}, f32[64,256]{1,0:T(8,128)S(1)}, u32[]{:S(2)}, u32[]{:S(2)}) collective-permute-start(f32[64,256]{1,0:T(8,128)S(1)} %add.25.first), channel_id=1, source_target_pairs={{0,16},{16,0},{1,17},{17,1},{2,18},{18,2},{3,19},{19,3},{4,20},{20... | collective-permute-start | bytes 196616 | tf_op jit(solution)/shard_map/ppermute | solution.py:175
  19.3 8.3 %collective-permute-start.6 = (bf16[512,128]{1,0:T(8,128)(2,1)S(1)}, bf16[512,128]{1,0:T(8,128)(2,1)S(1)}, u32[]{:S(2)}, u32[]{:S(2)}) collective-permute-start(bf16[512,128]{1,0:T(8,128)(2,1)S(1)} %expand.1.refs_4_), channel_id=1, source_target_pairs={{0,8},{4,12},{8,0},{12,4},{1,9},{5,13},{9,1},{13,5},{2,10},{6,14},... | collective-permute-start | bytes 393224 | tf_op jit(solution)/shard_map/ppermute | solution.py:189
  19.7 12.6 %collective-permute-start.8 = (bf16[512,128]{1,0:T(8,128)(2,1)S(1)}, bf16[512,128]{1,0:T(8,128)(2,1)S(1)}, u32[]{:S(2)}, u32[]{:S(2)}) collective-permute-start(bf16[512,128]{1,0:T(8,128)(2,1)S(1)} %expand.1.refs_4_), channel_id=1, source_target_pairs={{0,4},{4,0},{8,12},{12,8},{1,5},{5,1},{9,13},{13,9},{2,6},{6,2},{1... | collective-permute-start | bytes 393224 | tf_op jit(solution)/shard_map/ppermute | solution.py:189
  20.3 15.0 %collective-permute-start.7 = (bf16[1024,128]{1,0:T(8,128)(2,1)S(1)}, bf16[1024,128]{1,0:T(8,128)(2,1)S(1)}, u32[]{:S(2)}, u32[]{:S(2)}) collective-permute-start(bf16[1024,128]{1,0:T(8,128)(2,1)S(1)} %collective-permute-done.1.refs_2_), channel_id=1, source_target_pairs={{0,4},{4,0},{8,12},{12,8},{1,5},{5,1},{9,13},{13,9},{2,6},{6,2},{1... | collective-permute-start | bytes 786440 | tf_op jit(solution)/shard_map/ppermute | solution.py:189
  27.6 7.8 %collective-permute-start.9 = (bf16[512,128]{1,0:T(8,128)(2,1)S(1)}, bf16[512,128]{1,0:T(8,128)(2,1)S(1)}, u32[]{:S(2)}, u32[]{:S(2)}) collective-permute-start(bf16[512,128]{1,0:T(8,128)(2,1)S(1)} %collective-permute-done.6.refs_5_), channel_id=1, source_target_pairs={{0,4},{4,0},{8,12},{12,8},{1,5},{5,1},{9,13},{13,9},{2,6},{6,2},{1... | collective-permute-start | bytes 393224 | tf_op jit(solution)/shard_map/ppermute | solution.py:189
  36.5 6.2 %collective-permute-start.10 = (bf16[512,128]{1,0:T(8,128)(2,1)S(1)}, bf16[512,128]{1,0:T(8,128)(2,1)S(1)}, u32[]{:S(2)}, u32[]{:S(2)}) collective-permute-start(bf16[512,128]{1,0:T(8,128)(2,1)S(1)} %attend.12), channel_id=1, source_target_pairs={{0,16},{16,0},{1,17},{17,1},{2,18},{18,2},{3,19},{19,3},{4,20},{20... | collective-permute-start | bytes 393224 | tf_op jit(solution)/shard_map/ppermute | solution.py:215
  39.4 5.0 %collective-permute-start.11 = (bf16[512,128]{1,0:T(8,128)(2,1)S(1)}, bf16[512,128]{1,0:T(8,128)(2,1)S(1)}, u32[]{:S(2)}, u32[]{:S(2)}) collective-permute-start(bf16[512,128]{1,0:T(8,128)(2,1)S(1)} %attend.13), channel_id=1, source_target_pairs={{0,16},{16,0},{1,17},{17,1},{2,18},{18,2},{3,19},{19,3},{4,20},{20... | collective-permute-start | bytes 393224 | tf_op jit(solution)/shard_map/ppermute | solution.py:215
where the time goes:
time: 45.7 us; the launch traced here: 45.6 us
  waiting for transfers between devices  14.6 us (32%)
  starting transfers between devices  14.5 us (32%)
  Pallas kernels  13.1 us (29%)
  local copies, waits for them, and re-layouts  1.93 us (4%)
  other arithmetic  1.2 us (3%)
    pallas_call x7, Pallas kernels, attend(): pl.pallas_call(functools.partial(attend_kernel, span, masks, state is not...  11.3 us
    ppermute x6, starting transfers between devices, gather_blocks(): held[mask ^ step] = lax.ppermute(sent, 'blk', perm)  8.13 us
    ppermute x6, waiting for transfers between devices, gather_blocks(): held[mask ^ step] = lax.ppermute(sent, 'blk', perm)  6.38 us
    ppermute x3, waiting for transfers between devices, butterfly(): lax.ppermute(value, axis, [(i, i ^ step) for i in range(size)])  5.39 us
    ppermute x3, starting transfers between devices, swap(): return lax.ppermute(value, 'team', [(i, i ^ 1) for i in range(team_count)])  3.71 us
    ppermute x3, waiting for transfers between devices, swap(): return lax.ppermute(value, 'team', [(i, i ^ 1) for i in range(team_count)])  2.79 us
    ppermute x3, starting transfers between devices, butterfly(): lax.ppermute(value, axis, [(i, i ^ step) for i in range(size)])  2.66 us
    unnamed x26, local copies, waits for them, and re-layouts  1.17 us
  transfers between devices with their start and end apart: 12, of which 6 were waited for; matrix products, arithmetic and copies ran while one was open for 2% of the time, Pallas kernels for 26%

commit v1 on v0

--- a/solution.py
+++ b/solution.py
@@ -58,7 +58,7 @@
 
 def expand_kernel(ids_ref, first, second, key_up, value_up, key_base, value_base, out_ref):
     chosen = ids_ref[lax.axis_index("blk")]
-    latent = (first[...] + second[...]).astype(jnp.bfloat16)
+    latent = (first[...] + second[...].astype(jnp.float32)).astype(jnp.bfloat16)
     tokens = key_base.shape[0]
     for n, (up, base) in enumerate(((key_up, key_base), (value_up, value_base))):
         delta = lax.dot_general(
@@ -171,8 +171,9 @@
     step = 1
     pair = (value, None)
     while step < size:
-        value = pair[0] if pair[1] is None else pair[0] + pair[1]
-        pair = (value, lax.ppermute(value, axis, [(i, i ^ step) for i in range(size)]))
+        value = pair[0] if pair[1] is None else pair[0] + pair[1].astype(jnp.float32)
+        perm = [(i, i ^ step) for i in range(size)]
+        pair = (value, lax.ppermute(value.astype(jnp.bfloat16), axis, perm))
         step *= 2
     return pair
 
@@ -221,7 +222,7 @@
     latent, bounds = partial_latent(adapter_ids, block_order, features, jnp.swapaxes(adapter_down, 1, 2))
     own_prefix = pick(jnp.concatenate([prefix_key, prefix_value], axis=0), 1)
     first, second = butterfly(latent, "head", lax.axis_size("head"))
-    first, second = butterfly(first + second, "team", team_count)
+    first, second = butterfly(first + second.astype(jnp.float32), "team", team_count)
 
     prefix, _ = gather_blocks(own_prefix, block_count)
     own_queries = pick(queries, 1).reshape(rows, head_dim)
@@ -240,11 +241,12 @@
     own_state = attend(bounds, own_queries, None, early, False, group_dev, scale)
     new, own_state = gather_blocks(own_new, block_count, own_state)
     far_state = attend(bounds, far_queries, None, early, False, group_dev, scale)
-    middle = [(mask, new[mask]) for mask in new if mask in (0, block_count // 2)]
-    tail = [(None, prefix[last])]
-    tail += [(mask, new[mask]) for mask in new if mask not in (0, block_count // 2)]
-    far_state = attend(bounds, far_queries, far_state, middle, False, group_dev, scale)
+    half = block_count // 2
+    relayed = [(None, prefix[last])]
+    middle = [(mask, new[mask]) for mask in new if mask in (0, half)]
+    tail = [(mask, new[mask]) for mask in new if mask not in (0, half)]
     own_state = attend(bounds, own_queries, own_state, middle, False, group_dev, scale)
+    far_state = attend(bounds, far_queries, far_state, middle + relayed, False, group_dev, scale)
     far_state, own_state = lax.optimization_barrier((far_state, own_state))
     parts = 2 if rows % (2 * TILE) == 0 else 1
     part = rows // parts
@@ -253,7 +255,7 @@
         span = (n * part, part)
         out = attend(bounds, far_queries, far_state, tail, True, group_dev, scale, span)[0]
         received.append(swap(out))
-    own_out = attend(bounds, own_queries, own_state, tail, True, group_dev, scale)[0]
+    own_out = attend(bounds, own_queries, own_state, relayed + tail, True, group_dev, scale)[0]
     shape = (query_dev, 1, group_dev, head_dim)
     head = lax.broadcasted_iota(jnp.int32, queries.shape, 1)
     received = jnp.concatenate(received, axis=0)

time: 45.7 us -> 44.6 us (0.976)
  waiting for transfers between devices: 14.6 us -> 13.6 us
    ppermute x3, waiting for transfers between devices: 5.39 us -> 4.74 us  [butterfly(): pair = (value, lax.ppermute(value.astype(jnp.bfloat16), axis, perm))]
  transfers between devices with their start and end apart: 12 -> 12, of which waited for: 6 -> 6; matrix products, arithmetic and copies ran while one was open for 2% -> 2% of each run, Pallas kernels for 26% -> 28%
where the time goes in v1:
time: 44.6 us; the launch traced here: 44.5 us
  starting transfers between devices  14.5 us (33%)
  waiting for transfers between devices  13.6 us (30%)
  Pallas kernels  13 us (29%)
  local copies, waits for them, and re-layouts  1.93 us (4%)
  other arithmetic  1.21 us (3%)
    pallas_call x7, Pallas kernels, attend(): pl.pallas_call(functools.partial(attend_kernel, span, masks, state is not...  11.2 us
    ppermute x6, starting transfers between devices, gather_blocks(): held[mask ^ step] = lax.ppermute(sent, 'blk', perm)  8.13 us
    ppermute x6, waiting for transfers between devices, gather_blocks(): held[mask ^ step] = lax.ppermute(sent, 'blk', perm)  6.27 us
    ppermute x3, waiting for transfers between devices, butterfly(): pair = (value, lax.ppermute(value.astype(jnp.bfloat16), axis, perm))  4.74 us
    ppermute x3, starting transfers between devices, swap(): return lax.ppermute(value, 'team', [(i, i ^ 1) for i in range(team_count)])  3.71 us
    ppermute x3, starting transfers between devices, butterfly(): pair = (value, lax.ppermute(value.astype(jnp.bfloat16), axis, perm))  2.61 us
    ppermute x3, waiting for transfers between devices, swap(): return lax.ppermute(value, 'team', [(i, i ^ 1) for i in range(team_count)])  2.57 us
    unnamed x26, local copies, waits for them, and re-layouts  1.17 us
  transfers between devices with their start and end apart: 12, of which 6 were waited for; matrix products, arithmetic and copies ran while one was open for 2% of the time, Pallas kernels for 28%

profile of v1, /device:TPU:0, one launch (start us, length us, event | category | flops | bytes accessed | tf_op | source)
XLA Modules:
  0.0 44.5 jit_solution(13148892602522855111)
XLA Ops:
  0.0 1.0 %copy.12 = bf16[512,2,128]{2,0,1:T(8,128)(2,1)S(1)} copy(bf16[512,2,128]{2,1,0:T(2,128)(2,1)} %param.18) | data formatting | bytes 524288 | tf_op args[7]
  1.0 0.0 copy-start.1
  1.1 0.0 copy-start
  1.1 0.0 copy-start.2
  1.2 0.0 copy-start.3
  1.2 4.1 %collective-permute-start.1 = (bf16[1024,128]{1,0:T(8,128)(2,1)S(1)}, bf16[1024,128]{1,0:T(8,128)(2,1)S(1)}, u32[]{:S(2)}, u32[]{:S(2)}) collective-permute-start(bf16[1024,128]{1,0:T(8,128)(2,1)S(1)} %fusion.1.refs_1_), channel_id=1, source_target_pairs={{0,8},{4,12},{8,0},{12,4},{1,9},{5,13},{9,1},{13,5},{2,10},{6,14},... | collective-permute-start | bytes 786440 | tf_op jit(solution)/shard_map/ppermute | solution.py:190
  5.3 1.6 %collective-permute-start.2 = (bf16[1024,128]{1,0:T(8,128)(2,1)S(1)}, bf16[1024,128]{1,0:T(8,128)(2,1)S(1)}, u32[]{:S(2)}, u32[]{:S(2)}) collective-permute-start(bf16[1024,128]{1,0:T(8,128)(2,1)S(1)} %fusion.1.refs_1_), channel_id=1, source_target_pairs={{0,4},{4,0},{8,12},{12,8},{1,5},{5,1},{9,13},{13,9},{2,6},{6,2},{1... | collective-permute-start | bytes 786440 | tf_op jit(solution)/shard_map/ppermute | solution.py:190
  6.9 0.0 copy-done.3
  6.9 0.0 copy-start.4
  6.9 1.0 %partial_latent.1 = (f32[64,256]{1,0:T(8,128)S(1)}, s32[4,128]{1,0:T(4,128)S(1)}) custom-call(s32[4]{0:T(128)S(1)} %copy-done.2, s32[4]{0:T(128)S(1)} %copy-done.3, bf16[256,1024]{1,0:T(8,128)(2,1)S(1)} %copy-done, bf16[4,64,1024]{2,1,0:T(8,128)(2,1)S(1)} %bitcast.22), custom_call_target="tpu_custom_call" | custom-call | flops 33554432 | bytes 655360 | tf_op jit(solution)/shard_map/partial_latent/pallas_call | solution.py:40
  8.0 0.1 collective-permute-start.3
  8.0 0.0 copy-start.7
  8.1 0.2 constant_dynamic-slice_fusion.5
  8.3 0.0 copy-start.6
  8.3 1.6 %collective-permute-start = (bf16[1024,128]{1,0:T(8,128)(2,1)S(1)}, bf16[1024,128]{1,0:T(8,128)(2,1)S(1)}, u32[]{:S(2)}, u32[]{:S(2)}) collective-permute-start(bf16[1024,128]{1,0:T(8,128)(2,1)S(1)} %bitcast.29), channel_id=1, source_target_pairs={{0,16},{16,0},{1,17},{17,1},{2,18},{18,2},{3,19},{19,3},{4,20},{20... | collective-permute-start | bytes 786440 | tf_op jit(solution)/shard_map/ppermute | solution.py:216
  9.8 0.0 collective-permute-done.3
  9.8 1.6 %collective-permute-start.4 = (bf16[64,256]{1,0:T(8,128)(2,1)S(1)}, bf16[64,256]{1,0:T(8,128)(2,1)S(1)}, u32[]{:S(2)}, u32[]{:S(2)}) collective-permute-start(bf16[64,256]{1,0:T(8,128)(2,1)S(1)} %fusion.2), channel_id=1, source_target_pairs={{0,2},{1,3},{2,0},{3,1},{4,6},{5,7},{6,4},{7,5},{8,10},{9,11},{10,... | collective-permute-start | bytes 98312 | tf_op jit(solution)/shard_map/ppermute | solution.py:176
  11.4 0.3 constant_dynamic-slice_fusion
  11.7 0.0 copy-start.8
  11.7 2.1 %collective-permute-done.4 = bf16[64,256]{1,0:T(8,128)(2,1)S(1)} collective-permute-done((bf16[64,256]{1,0:T(8,128)(2,1)S(1)}, bf16[64,256]{1,0:T(8,128)(2,1)S(1)}, u32[]{:S(2)}, u32[]{:S(2)}) %collective-permute-start.4) | collective-permute-done | bytes 32800 | tf_op jit(solution)/shard_map/ppermute | solution.py:176
  13.8 1.0 %collective-permute-start.5 = (bf16[64,256]{1,0:T(8,128)(2,1)S(1)}, bf16[64,256]{1,0:T(8,128)(2,1)S(1)}, u32[]{:S(2)}, u32[]{:S(2)}) collective-permute-start(bf16[64,256]{1,0:T(8,128)(2,1)S(1)} %get-tuple-element.39), channel_id=1, source_target_pairs={{0,16},{16,0},{1,17},{17,1},{2,18},{18,2},{3,19},{19,3},{4,20},{20... | collective-permute-start | bytes 98312 | tf_op jit(solution)/shard_map/ppermute | solution.py:176
  14.8 0.0 copy-done.9
  14.8 0.3 constant_dynamic-slice_fusion.2
  15.2 2.6 %collective-permute-done.5.second = bf16[64,256]{1,0:T(8,128)(2,1)S(1)} collective-permute-done((bf16[64,256]{1,0:T(8,128)(2,1)S(1)}, bf16[64,256]{1,0:T(8,128)(2,1)S(1)}, u32[]{:S(2)}, u32[]{:S(2)}) %collective-permute-start.5) | collective-permute-done | bytes 32800 | tf_op jit(solution)/shard_map/ppermute | solution.py:176
  17.8 0.8 %expand.1.refs_4_ = bf16[512,128]{1,0:T(8,128)(2,1)S(1)} custom-call(s32[4]{0:T(128)S(1)} %copy-done.2, f32[64,256]{1,0:T(8,128)S(1)} %get-tuple-element.40.first, bf16[64,256]{1,0:T(8,128)(2,1)S(1)} %collective-permute-done.5.second, bf16[4,64,128]{2,1,0:T(8,128)(2,1)S(1)} %bitcast.26, bf16[4,64,128]{2,1,0:T(8,128)(2,1)S(1)} %bitcast.25, ...), custom_call_target="tpu_custom_call" | custom-call | flops 8388608 | bytes 262144 | tf_op jit(solution)/shard_map/expand/pallas_call | solution.py:74
  18.6 0.4 collective-permute-start.6
  19.0 0.7 %collective-permute-start.8 = (bf16[512,128]{1,0:T(8,128)(2,1)S(1)}, bf16[512,128]{1,0:T(8,128)(2,1)S(1)}, u32[]{:S(2)}, u32[]{:S(2)}) collective-permute-start(bf16[512,128]{1,0:T(8,128)(2,1)S(1)} %expand.1.refs_4_), channel_id=1, source_target_pairs={{0,4},{4,0},{8,12},{12,8},{1,5},{5,1},{9,13},{13,9},{2,6},{6,2},{1... | collective-permute-start | bytes 393224 | tf_op jit(solution)/shard_map/ppermute | solution.py:190
  19.6 0.0 collective-permute-done.1.refs_2_
  19.7 1.4 %collective-permute-start.7 = (bf16[1024,128]{1,0:T(8,128)(2,1)S(1)}, bf16[1024,128]{1,0:T(8,128)(2,1)S(1)}, u32[]{:S(2)}, u32[]{:S(2)}) collective-permute-start(bf16[1024,128]{1,0:T(8,128)(2,1)S(1)} %collective-permute-done.1.refs_2_), channel_id=1, source_target_pairs={{0,4},{4,0},{8,12},{12,8},{1,5},{5,1},{9,13},{13,9},{2,6},{6,2},{1... | collective-permute-start | bytes 786440 | tf_op jit(solution)/shard_map/ppermute | solution.py:190
  21.0 0.0 collective-permute-done.2.refs_3_
  21.0 2.5 %attend.9 = (f32[1024,128]{1,0:T(8,128)S(1)}, f32[1024,256]{1,0:T(8,128)S(1)}) custom-call(bf16[1024,128]{1,0:T(8,128)(2,1)S(1)} %bitcast.19, bf16[1024,128]{1,0:T(8,128)(2,1)S(1)} %fusion.1.refs_1_, bf16[1024,128]{1,0:T(8,128)(2,1)S(1)} %collective-permute-done.1.refs_2_, bf16[1024,128]{1,0:T(8,128)(2,1)S(1)} %collective-permute-done.2.refs_3_), custom_call_target="tpu_custom_call" | custom-call | flops 1207959552 | bytes 524288 | tf_op jit(solution)/shard_map/attend/pallas_call | solution.py:155
  23.5 3.7 %collective-permute-done.6.refs_5_ = bf16[512,128]{1,0:T(8,128)(2,1)S(1)} collective-permute-done((bf16[512,128]{1,0:T(8,128)(2,1)S(1)}, bf16[512,128]{1,0:T(8,128)(2,1)S(1)}, u32[]{:S(2)}, u32[]{:S(2)}) %collective-permute-start.6) | collective-permute-done | bytes 131104 | tf_op jit(solution)/shard_map/ppermute | solution.py:190
  27.2 0.0 collective-permute-start.9
  27.2 0.0 collective-permute-done.refs_0_.refs_1_
  27.2 2.5 %attend.7 = (f32[1024,128]{1,0:T(8,128)S(1)}, f32[1024,256]{1,0:T(8,128)S(1)}) custom-call(bf16[1024,128]{1,0:T(8,128)(2,1)S(1)} %collective-permute-done.refs_0_.refs_1_, bf16[1024,128]{1,0:T(8,128)(2,1)S(1)} %fusion.1.refs_1_, bf16[1024,128]{1,0:T(8,128)(2,1)S(1)} %collective-permute-done.1.refs_2_, bf16[1024,128]{1,0:T(8,128)(2,1)S(1)} %collective-permute-done.2.refs_3_), custom_call_target="tpu_custom_call" | custom-call | flops 1207959552 | bytes 524288 | tf_op jit(solution)/shard_map/attend/pallas_call | solution.py:155
  29.8 1.1 %attend.10 = (f32[1024,128]{1,0:T(8,128)S(1)}, f32[1024,256]{1,0:T(8,128)S(1)}) custom-call(s32[4,128]{1,0:T(4,128)S(1)} %get-tuple-element.22.refs_0_, bf16[1024,128]{1,0:T(8,128)(2,1)S(1)} %bitcast.20, f32[1024,128]{1,0:T(8,128)S(1)} %get-tuple-element.30.refs_2_, f32[1024,256]{1,0:T(8,128)S(1)} %get-tuple-element.31.refs_3_, ...), custom_call_target="tpu_custom_call" | custom-call | flops 402653184 | bytes 524288 | tf_op jit(solution)/shard_map/attend/pallas_call | solution.py:155
  30.9 2.5 %collective-permute-done.7.refs_6_.refs_4_ = bf16[1024,128]{1,0:T(8,128)(2,1)S(1)} collective-permute-done((bf16[1024,128]{1,0:T(8,128)(2,1)S(1)}, bf16[1024,128]{1,0:T(8,128)(2,1)S(1)}, u32[]{:S(2)}, u32[]{:S(2)}) %collective-permute-start.7) | collective-permute-done | bytes 262176 | tf_op jit(solution)/shard_map/ppermute | solution.py:190
  33.5 1.8 %attend.8 = (f32[1024,128]{1,0:T(8,128)S(1)}, f32[1024,256]{1,0:T(8,128)S(1)}) custom-call(s32[4,128]{1,0:T(4,128)S(1)} %get-tuple-element.22.refs_0_, bf16[1024,128]{1,0:T(8,128)(2,1)S(1)} %collective-permute-done.refs_0_.refs_1_, f32[1024,128]{1,0:T(8,128)S(1)} %get-tuple-element.23.refs_2_, f32[1024,256]{1,0:T(8,128)S(1)} %get-tuple-element.24.refs_3_, ...), custom_call_target="tpu_custom_call" | custom-call | flops 805306368 | bytes 524288 | tf_op jit(solution)/shard_map/attend/pallas_call | solution.py:155
  35.3 0.0 collective-permute-done.8.refs_5_.refs_4_
  35.3 0.0 collective-permute-done.9.refs_6_.refs_5_
  35.3 0.7 %attend.12 = bf16[512,128]{1,0:T(8,128)(2,1)S(1)} custom-call(s32[4,128]{1,0:T(4,128)S(1)} %get-tuple-element.22.refs_0_, bf16[1024,128]{1,0:T(8,128)(2,1)S(1)} %collective-permute-done.refs_0_.refs_1_, f32[1024,128]{1,0:T(8,128)S(1)} %get-tuple-element.37.refs_2_, f32[1024,256]{1,0:T(8,128)S(1)} %get-tuple-element.38.refs_3_, ...), custom_call_target="tpu_custom_call" | custom-call | flops 201326592 | bytes 262144 | tf_op jit(solution)/shard_map/attend/pallas_call | solution.py:155
  36.0 1.6 %collective-permute-start.10 = (bf16[512,128]{1,0:T(8,128)(2,1)S(1)}, bf16[512,128]{1,0:T(8,128)(2,1)S(1)}, u32[]{:S(2)}, u32[]{:S(2)}) collective-permute-start(bf16[512,128]{1,0:T(8,128)(2,1)S(1)} %attend.12), channel_id=1, source_target_pairs={{0,16},{16,0},{1,17},{17,1},{2,18},{18,2},{3,19},{19,3},{4,20},{20... | collective-permute-start | bytes 393224 | tf_op jit(solution)/shard_map/ppermute | solution.py:216
  37.6 0.7 %attend.13 = bf16[512,128]{1,0:T(8,128)(2,1)S(1)} custom-call(s32[4,128]{1,0:T(4,128)S(1)} %get-tuple-element.22.refs_0_, bf16[1024,128]{1,0:T(8,128)(2,1)S(1)} %collective-permute-done.refs_0_.refs_1_, f32[1024,128]{1,0:T(8,128)S(1)} %get-tuple-element.37.refs_2_, f32[1024,256]{1,0:T(8,128)S(1)} %get-tuple-element.38.refs_3_, ...), custom_call_target="tpu_custom_call" | custom-call | flops 201326592 | bytes 262144 | tf_op jit(solution)/shard_map/attend/pallas_call | solution.py:155
  38.3 0.6 %collective-permute-start.11 = (bf16[512,128]{1,0:T(8,128)(2,1)S(1)}, bf16[512,128]{1,0:T(8,128)(2,1)S(1)}, u32[]{:S(2)}, u32[]{:S(2)}) collective-permute-start(bf16[512,128]{1,0:T(8,128)(2,1)S(1)} %attend.13), channel_id=1, source_target_pairs={{0,16},{16,0},{1,17},{17,1},{2,18},{18,2},{3,19},{19,3},{4,20},{20... | collective-permute-start | bytes 393224 | tf_op jit(solution)/shard_map/ppermute | solution.py:216
  38.9 1.8 %attend.11 = bf16[1024,128]{1,0:T(8,128)(2,1)S(1)} custom-call(s32[4,128]{1,0:T(4,128)S(1)} %get-tuple-element.22.refs_0_, bf16[1024,128]{1,0:T(8,128)(2,1)S(1)} %bitcast.21, f32[1024,128]{1,0:T(8,128)S(1)} %get-tuple-element.34.refs_2_, f32[1024,256]{1,0:T(8,128)S(1)} %get-tuple-element.35.refs_3_, ...), custom_call_target="tpu_custom_call" | custom-call | flops 805306368 | bytes 524288 | tf_op jit(solution)/shard_map/attend/pallas_call | solution.py:155
  40.7 0.9 %collective-permute-done.10 = bf16[512,128]{1,0:T(8,128)(2,1)S(1)} collective-permute-done((bf16[512,128]{1,0:T(8,128)(2,1)S(1)}, bf16[512,128]{1,0:T(8,128)(2,1)S(1)}, u32[]{:S(2)}, u32[]{:S(2)}) %collective-permute-start.10) | collective-permute-done | bytes 131104 | tf_op jit(solution)/shard_map/ppermute | solution.py:216
  41.6 1.7 %collective-permute-done.11 = bf16[512,128]{1,0:T(8,128)(2,1)S(1)} collective-permute-done((bf16[512,128]{1,0:T(8,128)(2,1)S(1)}, bf16[512,128]{1,0:T(8,128)(2,1)S(1)}, u32[]{:S(2)}, u32[]{:S(2)}) %collective-permute-start.11) | collective-permute-done | bytes 131104 | tf_op jit(solution)/shard_map/ppermute | solution.py:216
  43.3 1.1 %broadcast_select_fusion = bf16[256,2,4,128]{3,2,1,0:T(4,128)(2,1)} fusion(pred[2]{0:T(512)(128)(4,1)S(1)} %iota_compare_fusion, bf16[256,4,128]{2,1,0:T(4,128)(2,1)S(1)} %bitcast.28, bf16[256,4,128]{2,1,0:T(4,128)(2,1)S(1)} %bitcast.27), kind=kLoop, calls=%fused_computation.2 | loop fusion | flops 262144 | bytes 1048578 | tf_op jit(solution)/shard_map/jit(_where)/select_n | solution.py:262
  (21 shorter events, 0.2 us)
Async XLA Ops:
  0.0 1.0 %copy-start.5 = (bf16[512,2,128]{2,1,0:T(2,128)(2,1)S(1)}, bf16[512,2,128]{2,1,0:T(2,128)(2,1)}, u32[]{:S(2)}) copy-start(bf16[512,2,128]{2,1,0:T(2,128)(2,1)} %param.19) | copy-start | bytes 786436
  1.0 5.8 %copy-start.1 = (bf16[4,1024,64]{1,2,0:T(8,128)(2,1)S(1)}, bf16[4,1024,64]{1,2,0:T(8,128)(2,1)}, u32[]{:S(2)}) copy-start(bf16[4,1024,64]{1,2,0:T(8,128)(2,1)} %param.13) | copy-start | bytes 1572868
  1.1 5.8 %copy-start = (bf16[256,1024]{1,0:T(8,128)(2,1)S(1)}, bf16[256,1024]{1,0:T(8,128)(2,1)}, u32[]{:S(2)}) copy-start(bf16[256,1024]{1,0:T(8,128)(2,1)} %features_ref.1) | copy-start | bytes 1572868
  1.1 5.7 %copy-start.2 = (s32[4]{0:T(128)S(1)}, s32[4]{0:T(128)}, u32[]{:S(2)}) copy-start(s32[4]{0:T(128)} %ids_ref.3) | copy-start | bytes 52
  1.2 5.7 %copy-start.3 = (s32[4]{0:T(128)S(1)}, s32[4]{0:T(128)}, u32[]{:S(2)}) copy-start(s32[4]{0:T(128)} %order_ref.1) | copy-start | bytes 52
  1.2 18.5 %collective-permute-start.1 = (bf16[1024,128]{1,0:T(8,128)(2,1)S(1)}, bf16[1024,128]{1,0:T(8,128)(2,1)S(1)}, u32[]{:S(2)}, u32[]{:S(2)}) collective-permute-start(bf16[1024,128]{1,0:T(8,128)(2,1)S(1)} %fusion.1.refs_1_), channel_id=1, source_target_pairs={{0,8},{4,12},{8,0},{12,4},{1,9},{5,13},{9,1},{13,5},{2,10},{6,14},... | collective-permute-start | bytes 786440 | tf_op jit(solution)/shard_map/ppermute | solution.py:190
  5.3 15.7 %collective-permute-start.2 = (bf16[1024,128]{1,0:T(8,128)(2,1)S(1)}, bf16[1024,128]{1,0:T(8,128)(2,1)S(1)}, u32[]{:S(2)}, u32[]{:S(2)}) collective-permute-start(bf16[1024,128]{1,0:T(8,128)(2,1)S(1)} %fusion.1.refs_1_), channel_id=1, source_target_pairs={{0,4},{4,0},{8,12},{12,8},{1,5},{5,1},{9,13},{13,9},{2,6},{6,2},{1... | collective-permute-start | bytes 786440 | tf_op jit(solution)/shard_map/ppermute | solution.py:190
  6.9 1.1 %copy-start.4 = (bf16[256,2,4,128]{3,2,1,0:T(4,128)(2,1)S(1)}, bf16[256,2,4,128]{3,2,1,0:T(4,128)(2,1)}, u32[]{:S(2)}) copy-start(bf16[256,2,4,128]{3,2,1,0:T(4,128)(2,1)} %param.11) | copy-start | bytes 1572868
  8.0 1.9 %collective-permute-start.3 = (bf16[64,256]{1,0:T(8,128)(2,1)S(1)}, bf16[64,256]{1,0:T(8,128)(2,1)S(1)}, u32[]{:S(2)}, u32[]{:S(2)}) collective-permute-start(bf16[64,256]{1,0:T(8,128)(2,1)S(1)} %convert_element_type.15), channel_id=1, source_target_pairs={{0,1},{1,0},{2,3},{3,2},{4,5},{5,4},{6,7},{7,6},{8,9},{9,8},{10,11... | collective-permute-start | bytes 98312 | tf_op jit(solution)/shard_map/ppermute | solution.py:176
  8.0 3.4 %copy-start.7 = (bf16[256,2,128]{2,1,0:T(2,128)(2,1)S(1)}, bf16[256,2,128]{2,1,0:T(2,128)(2,1)}, u32[]{:S(2)}) copy-start(bf16[256,2,128]{2,1,0:T(2,128)(2,1)} %param.16) | copy-start | bytes 393220
  8.3 3.2 %copy-start.6 = (bf16[256,2,128]{2,1,0:T(2,128)(2,1)S(1)}, bf16[256,2,128]{2,1,0:T(2,128)(2,1)}, u32[]{:S(2)}) copy-start(bf16[256,2,128]{2,1,0:T(2,128)(2,1)} %param.17) | copy-start | bytes 393220
  8.3 19.0 %collective-permute-start = (bf16[1024,128]{1,0:T(8,128)(2,1)S(1)}, bf16[1024,128]{1,0:T(8,128)(2,1)S(1)}, u32[]{:S(2)}, u32[]{:S(2)}) collective-permute-start(bf16[1024,128]{1,0:T(8,128)(2,1)S(1)} %bitcast.29), channel_id=1, source_target_pairs={{0,16},{16,0},{1,17},{17,1},{2,18},{18,2},{3,19},{19,3},{4,20},{20... | collective-permute-start | bytes 786440 | tf_op jit(solution)/shard_map/ppermute | solution.py:216
  9.8 4.0 %collective-permute-start.4 = (bf16[64,256]{1,0:T(8,128)(2,1)S(1)}, bf16[64,256]{1,0:T(8,128)(2,1)S(1)}, u32[]{:S(2)}, u32[]{:S(2)}) collective-permute-start(bf16[64,256]{1,0:T(8,128)(2,1)S(1)} %fusion.2), channel_id=1, source_target_pairs={{0,2},{1,3},{2,0},{3,1},{4,6},{5,7},{6,4},{7,5},{8,10},{9,11},{10,... | collective-permute-start | bytes 98312 | tf_op jit(solution)/shard_map/ppermute | solution.py:176
  11.4 3.4 %copy-start.9 = (bf16[4,64,2,128]{3,2,1,0:T(2,128)(2,1)S(1)}, bf16[4,64,2,128]{3,2,1,0:T(2,128)(2,1)}, u32[]{:S(2)}) copy-start(bf16[4,64,2,128]{3,2,1,0:T(2,128)(2,1)} %param.14) | copy-start | bytes 393220
  11.7 3.1 %copy-start.8 = (bf16[4,64,2,128]{3,2,1,0:T(2,128)(2,1)S(1)}, bf16[4,64,2,128]{3,2,1,0:T(2,128)(2,1)}, u32[]{:S(2)}) copy-start(bf16[4,64,2,128]{3,2,1,0:T(2,128)(2,1)} %param.15) | copy-start | bytes 393220
  13.8 4.0 %collective-permute-start.5 = (bf16[64,256]{1,0:T(8,128)(2,1)S(1)}, bf16[64,256]{1,0:T(8,128)(2,1)S(1)}, u32[]{:S(2)}, u32[]{:S(2)}) collective-permute-start(bf16[64,256]{1,0:T(8,128)(2,1)S(1)} %get-tuple-element.39), channel_id=1, source_target_pairs={{0,16},{16,0},{1,17},{17,1},{2,18},{18,2},{3,19},{19,3},{4,20},{20... | collective-permute-start | bytes 98312 | tf_op jit(solution)/shard_map/ppermute | solution.py:176
  18.6 8.7 %collective-permute-start.6 = (bf16[512,128]{1,0:T(8,128)(2,1)S(1)}, bf16[512,128]{1,0:T(8,128)(2,1)S(1)}, u32[]{:S(2)}, u32[]{:S(2)}) collective-permute-start(bf16[512,128]{1,0:T(8,128)(2,1)S(1)} %expand.1.refs_4_), channel_id=1, source_target_pairs={{0,8},{4,12},{8,0},{12,4},{1,9},{5,13},{9,1},{13,5},{2,10},{6,14},... | collective-permute-start | bytes 393224 | tf_op jit(solution)/shard_map/ppermute | solution.py:190
  19.0 16.3 %collective-permute-start.8 = (bf16[512,128]{1,0:T(8,128)(2,1)S(1)}, bf16[512,128]{1,0:T(8,128)(2,1)S(1)}, u32[]{:S(2)}, u32[]{:S(2)}) collective-permute-start(bf16[512,128]{1,0:T(8,128)(2,1)S(1)} %expand.1.refs_4_), channel_id=1, source_target_pairs={{0,4},{4,0},{8,12},{12,8},{1,5},{5,1},{9,13},{13,9},{2,6},{6,2},{1... | collective-permute-start | bytes 393224 | tf_op jit(solution)/shard_map/ppermute | solution.py:190
  19.7 13.8 %collective-permute-start.7 = (bf16[1024,128]{1,0:T(8,128)(2,1)S(1)}, bf16[1024,128]{1,0:T(8,128)(2,1)S(1)}, u32[]{:S(2)}, u32[]{:S(2)}) collective-permute-start(bf16[1024,128]{1,0:T(8,128)(2,1)S(1)} %collective-permute-done.1.refs_2_), channel_id=1, source_target_pairs={{0,4},{4,0},{8,12},{12,8},{1,5},{5,1},{9,13},{13,9},{2,6},{6,2},{1... | collective-permute-start | bytes 786440 | tf_op jit(solution)/shard_map/ppermute | solution.py:190
  27.2 8.0 %collective-permute-start.9 = (bf16[512,128]{1,0:T(8,128)(2,1)S(1)}, bf16[512,128]{1,0:T(8,128)(2,1)S(1)}, u32[]{:S(2)}, u32[]{:S(2)}) collective-permute-start(bf16[512,128]{1,0:T(8,128)(2,1)S(1)} %collective-permute-done.6.refs_5_), channel_id=1, source_target_pairs={{0,4},{4,0},{8,12},{12,8},{1,5},{5,1},{9,13},{13,9},{2,6},{6,2},{1... | collective-permute-start | bytes 393224 | tf_op jit(solution)/shard_map/ppermute | solution.py:190
  36.0 5.6 %collective-permute-start.10 = (bf16[512,128]{1,0:T(8,128)(2,1)S(1)}, bf16[512,128]{1,0:T(8,128)(2,1)S(1)}, u32[]{:S(2)}, u32[]{:S(2)}) collective-permute-start(bf16[512,128]{1,0:T(8,128)(2,1)S(1)} %attend.12), channel_id=1, source_target_pairs={{0,16},{16,0},{1,17},{17,1},{2,18},{18,2},{3,19},{19,3},{4,20},{20... | collective-permute-start | bytes 393224 | tf_op jit(solution)/shard_map/ppermute | solution.py:216
  38.3 5.0 %collective-permute-start.11 = (bf16[512,128]{1,0:T(8,128)(2,1)S(1)}, bf16[512,128]{1,0:T(8,128)(2,1)S(1)}, u32[]{:S(2)}, u32[]{:S(2)}) collective-permute-start(bf16[512,128]{1,0:T(8,128)(2,1)S(1)} %attend.13), channel_id=1, source_target_pairs={{0,16},{16,0},{1,17},{17,1},{2,18},{18,2},{3,19},{19,3},{4,20},{20... | collective-permute-start | bytes 393224 | tf_op jit(solution)/shard_map/ppermute | solution.py:216

commit v2 on v1

--- a/solution.py
+++ b/solution.py
@@ -58,7 +58,7 @@
 
 def expand_kernel(ids_ref, first, second, key_up, value_up, key_base, value_base, out_ref):
     chosen = ids_ref[lax.axis_index("blk")]
-    latent = (first[...] + second[...].astype(jnp.float32)).astype(jnp.bfloat16)
+    latent = (first[...] + second[...]).astype(jnp.bfloat16)
     tokens = key_base.shape[0]
     for n, (up, base) in enumerate(((key_up, key_base), (value_up, value_base))):
         delta = lax.dot_general(
@@ -171,9 +171,9 @@
     step = 1
     pair = (value, None)
     while step < size:
-        value = pair[0] if pair[1] is None else pair[0] + pair[1].astype(jnp.float32)
+        value = pair[0] if pair[1] is None else pair[0] + pair[1]
         perm = [(i, i ^ step) for i in range(size)]
-        pair = (value, lax.ppermute(value.astype(jnp.bfloat16), axis, perm))
+        pair = (value, lax.ppermute(value, axis, perm))
         step *= 2
     return pair
 
@@ -222,7 +222,7 @@
     latent, bounds = partial_latent(adapter_ids, block_order, features, jnp.swapaxes(adapter_down, 1, 2))
     own_prefix = pick(jnp.concatenate([prefix_key, prefix_value], axis=0), 1)
     first, second = butterfly(latent, "head", lax.axis_size("head"))
-    first, second = butterfly(first + second.astype(jnp.float32), "team", team_count)
+    first, second = butterfly(first + second, "team", team_count)
 
     prefix, _ = gather_blocks(own_prefix, block_count)
     own_queries = pick(queries, 1).reshape(rows, head_dim)
@@ -248,12 +248,14 @@
     own_state = attend(bounds, own_queries, own_state, middle, False, group_dev, scale)
     far_state = attend(bounds, far_queries, far_state, middle + relayed, False, group_dev, scale)
     far_state, own_state = lax.optimization_barrier((far_state, own_state))
-    parts = 2 if rows % (2 * TILE) == 0 else 1
+    near = [(mask, piece) for mask, piece in tail if mask != last]
+    far_state = attend(bounds, far_queries, far_state, near, False, group_dev, scale)
+    parts = 1
     part = rows // parts
     received = []
     for n in range(parts):
         span = (n * part, part)
-        out = attend(bounds, far_queries, far_state, tail, True, group_dev, scale, span)[0]
+        out = attend(bounds, far_queries, far_state, tail[-1:], True, group_dev, scale, span)[0]
         received.append(swap(out))
     own_out = attend(bounds, own_queries, own_state, relayed + tail, True, group_dev, scale)[0]
     shape = (query_dev, 1, group_dev, head_dim)

time: 44.6 us -> 44.9 us (level)
  waiting for transfers between devices: 13.6 us -> 14.3 us
    ppermute x3, waiting for transfers between devices: 4.74 us -> 5.39 us  [butterfly(): pair = (value, lax.ppermute(value, axis, perm))]
    ppermute x3 -> x2, starting transfers between devices: 3.71 us -> 3.33 us  [swap(): return lax.ppermute(value, 'team', [(i, i ^ 1) for i in range(team_count)])]
    ppermute x3 -> x2, waiting for transfers between devices: 2.57 us -> 2.81 us  [swap(): return lax.ppermute(value, 'team', [(i, i ^ 1) for i in range(team_count)])]
  transfers between devices with their start and end apart: 12 -> 11, of which waited for: 6 -> 5; matrix products, arithmetic and copies ran while one was open for 2% -> 2% of each run, Pallas kernels for 28% -> 27%
where the time goes in v2:
time: 44.9 us; the launch traced here: 44.8 us
  waiting for transfers between devices  14.3 us (32%)
  starting transfers between devices  14.1 us (31%)
  Pallas kernels  13 us (29%)
  local copies, waits for them, and re-layouts  1.93 us (4%)
  other arithmetic  1.18 us (3%)
    pallas_call x7, Pallas kernels, attend(): pl.pallas_call(functools.partial(attend_kernel, span, masks, state is not...  11.2 us
    ppermute x6, starting transfers between devices, gather_blocks(): held[mask ^ step] = lax.ppermute(sent, 'blk', perm)  8.13 us
    ppermute x6, waiting for transfers between devices, gather_blocks(): held[mask ^ step] = lax.ppermute(sent, 'blk', perm)  6.08 us
    ppermute x3, waiting for transfers between devices, butterfly(): pair = (value, lax.ppermute(value, axis, perm))  5.39 us
    ppermute x2, starting transfers between devices, swap(): return lax.ppermute(value, 'team', [(i, i ^ 1) for i in range(team_count)])  3.33 us
    ppermute x2, waiting for transfers between devices, swap(): return lax.ppermute(value, 'team', [(i, i ^ 1) for i in range(team_count)])  2.81 us
    ppermute x3, starting transfers between devices, butterfly(): pair = (value, lax.ppermute(value, axis, perm))  2.66 us
    unnamed x26, local copies, waits for them, and re-layouts  1.17 us
  transfers between devices with their start and end apart: 11, of which 5 were waited for; matrix products, arithmetic and copies ran while one was open for 2% of the time, Pallas kernels for 27%

profile of v2, /device:TPU:0, one launch (start us, length us, event | category | flops | bytes accessed | tf_op | source)
XLA Modules:
  0.0 44.8 jit_solution(17915229305458036554)
XLA Ops:
  0.0 1.0 %copy.12 = bf16[512,2,128]{2,0,1:T(8,128)(2,1)S(1)} copy(bf16[512,2,128]{2,1,0:T(2,128)(2,1)} %param.18) | data formatting | bytes 524288 | tf_op args[7]
  1.0 0.0 copy-start.1
  1.1 0.0 copy-start
  1.1 0.0 copy-start.2
  1.2 0.0 copy-start.3
  1.2 4.1 %collective-permute-start.1 = (bf16[1024,128]{1,0:T(8,128)(2,1)S(1)}, bf16[1024,128]{1,0:T(8,128)(2,1)S(1)}, u32[]{:S(2)}, u32[]{:S(2)}) collective-permute-start(bf16[1024,128]{1,0:T(8,128)(2,1)S(1)} %fusion.1.refs_1_), channel_id=1, source_target_pairs={{0,8},{4,12},{8,0},{12,4},{1,9},{5,13},{9,1},{13,5},{2,10},{6,14},... | collective-permute-start | bytes 786440 | tf_op jit(solution)/shard_map/ppermute | solution.py:190
  5.3 1.6 %collective-permute-start.2 = (bf16[1024,128]{1,0:T(8,128)(2,1)S(1)}, bf16[1024,128]{1,0:T(8,128)(2,1)S(1)}, u32[]{:S(2)}, u32[]{:S(2)}) collective-permute-start(bf16[1024,128]{1,0:T(8,128)(2,1)S(1)} %fusion.1.refs_1_), channel_id=1, source_target_pairs={{0,4},{4,0},{8,12},{12,8},{1,5},{5,1},{9,13},{13,9},{2,6},{6,2},{1... | collective-permute-start | bytes 786440 | tf_op jit(solution)/shard_map/ppermute | solution.py:190
  6.9 0.0 copy-done.3
  6.9 0.0 copy-start.4
  6.9 1.0 %partial_latent.1 = (f32[64,256]{1,0:T(8,128)S(1)}, s32[4,128]{1,0:T(4,128)S(1)}) custom-call(s32[4]{0:T(128)S(1)} %copy-done.2, s32[4]{0:T(128)S(1)} %copy-done.3, bf16[256,1024]{1,0:T(8,128)(2,1)S(1)} %copy-done, bf16[4,64,1024]{2,1,0:T(8,128)(2,1)S(1)} %bitcast.22), custom_call_target="tpu_custom_call" | custom-call | flops 33554432 | bytes 655360 | tf_op jit(solution)/shard_map/partial_latent/pallas_call | solution.py:40
  7.9 0.1 collective-permute-start.3
  8.0 0.0 copy-done.4
  8.0 0.0 copy-start.7
  8.0 0.2 constant_dynamic-slice_fusion.5
  8.2 0.0 copy-start.6
  8.3 1.6 %collective-permute-start = (bf16[1024,128]{1,0:T(8,128)(2,1)S(1)}, bf16[1024,128]{1,0:T(8,128)(2,1)S(1)}, u32[]{:S(2)}, u32[]{:S(2)}) collective-permute-start(bf16[1024,128]{1,0:T(8,128)(2,1)S(1)} %bitcast.28), channel_id=1, source_target_pairs={{0,16},{16,0},{1,17},{17,1},{2,18},{18,2},{3,19},{19,3},{4,20},{20... | collective-permute-start | bytes 786440 | tf_op jit(solution)/shard_map/ppermute | solution.py:216
  9.8 0.0 collective-permute-done.3
  9.8 1.6 %collective-permute-start.4 = (f32[64,256]{1,0:T(8,128)S(1)}, f32[64,256]{1,0:T(8,128)S(1)}, u32[]{:S(2)}, u32[]{:S(2)}) collective-permute-start(f32[64,256]{1,0:T(8,128)S(1)} %add.24), channel_id=1, source_target_pairs={{0,2},{1,3},{2,0},{3,1},{4,6},{5,7},{6,4},{7,5},{8,10},{9,11},{10,... | collective-permute-start | bytes 196616 | tf_op jit(solution)/shard_map/ppermute | solution.py:176
  11.4 0.0 copy-done.7
  11.4 0.3 constant_dynamic-slice_fusion
  11.7 0.0 copy-start.9
  11.7 0.0 copy-start.8
  11.8 2.4 %collective-permute-done.4 = f32[64,256]{1,0:T(8,128)S(1)} collective-permute-done((f32[64,256]{1,0:T(8,128)S(1)}, f32[64,256]{1,0:T(8,128)S(1)}, u32[]{:S(2)}, u32[]{:S(2)}) %collective-permute-start.4) | collective-permute-done | bytes 65568 | tf_op jit(solution)/shard_map/ppermute | solution.py:176
  14.2 1.0 %collective-permute-start.5 = (f32[64,256]{1,0:T(8,128)S(1)}, f32[64,256]{1,0:T(8,128)S(1)}, u32[]{:S(2)}, u32[]{:S(2)}) collective-permute-start(f32[64,256]{1,0:T(8,128)S(1)} %add.25.first), channel_id=1, source_target_pairs={{0,16},{16,0},{1,17},{17,1},{2,18},{18,2},{3,19},{19,3},{4,20},{20... | collective-permute-start | bytes 196616 | tf_op jit(solution)/shard_map/ppermute | solution.py:176
  15.2 0.3 constant_dynamic-slice_fusion.2
  15.5 3.0 %collective-permute-done.5.second = f32[64,256]{1,0:T(8,128)S(1)} collective-permute-done((f32[64,256]{1,0:T(8,128)S(1)}, f32[64,256]{1,0:T(8,128)S(1)}, u32[]{:S(2)}, u32[]{:S(2)}) %collective-permute-start.5) | collective-permute-done | bytes 65568 | tf_op jit(solution)/shard_map/ppermute | solution.py:176
  18.5 0.8 %expand.1.refs_4_ = bf16[512,128]{1,0:T(8,128)(2,1)S(1)} custom-call(s32[4]{0:T(128)S(1)} %copy-done.2, f32[64,256]{1,0:T(8,128)S(1)} %add.25.first, f32[64,256]{1,0:T(8,128)S(1)} %collective-permute-done.5.second, bf16[4,64,128]{2,1,0:T(8,128)(2,1)S(1)} %bitcast.26, bf16[4,64,128]{2,1,0:T(8,128)(2,1)S(1)} %bitcast.25, bf16[256,128]{1,0:T(8,128)(2,1)S(1)} %bitcast.24, ...), custom_call_target="tpu_custom_call" | custom-call | flops 8388608 | bytes 262144 | tf_op jit(solution)/shard_map/expand/pallas_call | solution.py:74
  19.3 0.4 collective-permute-start.6
  19.7 0.7 %collective-permute-start.8 = (bf16[512,128]{1,0:T(8,128)(2,1)S(1)}, bf16[512,128]{1,0:T(8,128)(2,1)S(1)}, u32[]{:S(2)}, u32[]{:S(2)}) collective-permute-start(bf16[512,128]{1,0:T(8,128)(2,1)S(1)} %expand.1.refs_4_), channel_id=1, source_target_pairs={{0,4},{4,0},{8,12},{12,8},{1,5},{5,1},{9,13},{13,9},{2,6},{6,2},{1... | collective-permute-start | bytes 393224 | tf_op jit(solution)/shard_map/ppermute | solution.py:190
  20.3 0.0 collective-permute-done.1.refs_2_
  20.3 1.4 %collective-permute-start.7 = (bf16[1024,128]{1,0:T(8,128)(2,1)S(1)}, bf16[1024,128]{1,0:T(8,128)(2,1)S(1)}, u32[]{:S(2)}, u32[]{:S(2)}) collective-permute-start(bf16[1024,128]{1,0:T(8,128)(2,1)S(1)} %collective-permute-done.1.refs_2_), channel_id=1, source_target_pairs={{0,4},{4,0},{8,12},{12,8},{1,5},{5,1},{9,13},{13,9},{2,6},{6,2},{1... | collective-permute-start | bytes 786440 | tf_op jit(solution)/shard_map/ppermute | solution.py:190
  21.7 0.0 collective-permute-done.2.refs_3_
  21.7 2.5 %attend.9 = (f32[1024,128]{1,0:T(8,128)S(1)}, f32[1024,256]{1,0:T(8,128)S(1)}) custom-call(bf16[1024,128]{1,0:T(8,128)(2,1)S(1)} %bitcast.19, bf16[1024,128]{1,0:T(8,128)(2,1)S(1)} %fusion.1.refs_1_, bf16[1024,128]{1,0:T(8,128)(2,1)S(1)} %collective-permute-done.1.refs_2_, bf16[1024,128]{1,0:T(8,128)(2,1)S(1)} %collective-permute-done.2.refs_3_), custom_call_target="tpu_custom_call" | custom-call | flops 1207959552 | bytes 524288 | tf_op jit(solution)/shard_map/attend/pallas_call | solution.py:155
  24.2 0.0 collective-permute-done.refs_0_.refs_1_
  24.2 2.5 %attend.7 = (f32[1024,128]{1,0:T(8,128)S(1)}, f32[1024,256]{1,0:T(8,128)S(1)}) custom-call(bf16[1024,128]{1,0:T(8,128)(2,1)S(1)} %collective-permute-done.refs_0_.refs_1_, bf16[1024,128]{1,0:T(8,128)(2,1)S(1)} %fusion.1.refs_1_, bf16[1024,128]{1,0:T(8,128)(2,1)S(1)} %collective-permute-done.1.refs_2_, bf16[1024,128]{1,0:T(8,128)(2,1)S(1)} %collective-permute-done.2.refs_3_), custom_call_target="tpu_custom_call" | custom-call | flops 1207959552 | bytes 524288 | tf_op jit(solution)/shard_map/attend/pallas_call | solution.py:155
  26.7 0.9 %collective-permute-done.6.refs_5_ = bf16[512,128]{1,0:T(8,128)(2,1)S(1)} collective-permute-done((bf16[512,128]{1,0:T(8,128)(2,1)S(1)}, bf16[512,128]{1,0:T(8,128)(2,1)S(1)}, u32[]{:S(2)}, u32[]{:S(2)}) %collective-permute-start.6) | collective-permute-done | bytes 131104 | tf_op jit(solution)/shard_map/ppermute | solution.py:190
  27.6 0.0 collective-permute-start.9
  27.6 1.1 %attend.10 = (f32[1024,128]{1,0:T(8,128)S(1)}, f32[1024,256]{1,0:T(8,128)S(1)}) custom-call(s32[4,128]{1,0:T(4,128)S(1)} %get-tuple-element.24.refs_0_, bf16[1024,128]{1,0:T(8,128)(2,1)S(1)} %bitcast.20, f32[1024,128]{1,0:T(8,128)S(1)} %get-tuple-element.32.refs_2_, f32[1024,256]{1,0:T(8,128)S(1)} %get-tuple-element.33.refs_3_, ...), custom_call_target="tpu_custom_call" | custom-call | flops 402653184 | bytes 524288 | tf_op jit(solution)/shard_map/attend/pallas_call | solution.py:155
  28.7 5.2 %collective-permute-done.7.refs_6_.refs_4_ = bf16[1024,128]{1,0:T(8,128)(2,1)S(1)} collective-permute-done((bf16[1024,128]{1,0:T(8,128)(2,1)S(1)}, bf16[1024,128]{1,0:T(8,128)(2,1)S(1)}, u32[]{:S(2)}, u32[]{:S(2)}) %collective-permute-start.7) | collective-permute-done | bytes 262176 | tf_op jit(solution)/shard_map/ppermute | solution.py:190
  33.9 1.8 %attend.8 = (f32[1024,128]{1,0:T(8,128)S(1)}, f32[1024,256]{1,0:T(8,128)S(1)}) custom-call(s32[4,128]{1,0:T(4,128)S(1)} %get-tuple-element.24.refs_0_, bf16[1024,128]{1,0:T(8,128)(2,1)S(1)} %collective-permute-done.refs_0_.refs_1_, f32[1024,128]{1,0:T(8,128)S(1)} %get-tuple-element.25.refs_2_, f32[1024,256]{1,0:T(8,128)S(1)} %get-tuple-element.26.refs_3_, ...), custom_call_target="tpu_custom_call" | custom-call | flops 805306368 | bytes 524288 | tf_op jit(solution)/shard_map/attend/pallas_call | solution.py:155
  35.7 0.0 collective-permute-done.8.refs_5_.refs_4_
  35.8 0.7 %attend.12 = (f32[1024,128]{1,0:T(8,128)S(1)}, f32[1024,256]{1,0:T(8,128)S(1)}) custom-call(s32[4,128]{1,0:T(4,128)S(1)} %get-tuple-element.24.refs_0_, bf16[1024,128]{1,0:T(8,128)(2,1)S(1)} %collective-permute-done.refs_0_.refs_1_, f32[1024,128]{1,0:T(8,128)S(1)} %get-tuple-element.39.refs_2_, f32[1024,256]{1,0:T(8,128)S(1)} %get-tuple-element.40.refs_3_, ...), custom_call_target="tpu_custom_call" | custom-call | flops 201326592 | bytes 524288 | tf_op jit(solution)/shard_map/attend/pallas_call | solution.py:155
  36.5 0.0 collective-permute-done.9.refs_6_.refs_4_
  36.5 0.7 %attend.13 = bf16[1024,128]{1,0:T(8,128)(2,1)S(1)} custom-call(s32[4,128]{1,0:T(4,128)S(1)} %get-tuple-element.24.refs_0_, bf16[1024,128]{1,0:T(8,128)(2,1)S(1)} %collective-permute-done.refs_0_.refs_1_, f32[1024,128]{1,0:T(8,128)S(1)} %get-tuple-element.41.refs_2_, f32[1024,256]{1,0:T(8,128)S(1)} %get-tuple-element.42.refs_3_, ...), custom_call_target="tpu_custom_call" | custom-call | flops 201326592 | bytes 524288 | tf_op jit(solution)/shard_map/attend/pallas_call | solution.py:155
  37.2 1.8 %collective-permute-start.10 = (bf16[1024,128]{1,0:T(8,128)(2,1)S(1)}, bf16[1024,128]{1,0:T(8,128)(2,1)S(1)}, u32[]{:S(2)}, u32[]{:S(2)}) collective-permute-start(bf16[1024,128]{1,0:T(8,128)(2,1)S(1)} %attend.13), channel_id=1, source_target_pairs={{0,16},{16,0},{1,17},{17,1},{2,18},{18,2},{3,19},{19,3},{4,20},{20... | collective-permute-start | bytes 786440 | tf_op jit(solution)/shard_map/ppermute | solution.py:216
  39.0 1.8 %attend.11 = bf16[1024,128]{1,0:T(8,128)(2,1)S(1)} custom-call(s32[4,128]{1,0:T(4,128)S(1)} %get-tuple-element.24.refs_0_, bf16[1024,128]{1,0:T(8,128)(2,1)S(1)} %bitcast.21, f32[1024,128]{1,0:T(8,128)S(1)} %get-tuple-element.36.refs_2_, f32[1024,256]{1,0:T(8,128)S(1)} %get-tuple-element.37.refs_3_, ...), custom_call_target="tpu_custom_call" | custom-call | flops 805306368 | bytes 524288 | tf_op jit(solution)/shard_map/attend/pallas_call | solution.py:155
  40.9 2.8 %collective-permute-done.10 = bf16[1024,128]{1,0:T(8,128)(2,1)S(1)} collective-permute-done((bf16[1024,128]{1,0:T(8,128)(2,1)S(1)}, bf16[1024,128]{1,0:T(8,128)(2,1)S(1)}, u32[]{:S(2)}, u32[]{:S(2)}) %collective-permute-start.10) | collective-permute-done | bytes 262176 | tf_op jit(solution)/shard_map/ppermute | solution.py:216
  43.7 1.1 %broadcast_select_fusion = bf16[256,2,4,128]{3,2,1,0:T(4,128)(2,1)} fusion(pred[2]{0:T(512)(128)(4,1)S(1)} %iota_compare_fusion, bf16[256,4,128]{2,1,0:T(4,128)(2,1)S(1)} %bitcast.29, bf16[256,4,128]{2,1,0:T(4,128)(2,1)S(1)} %bitcast.27), kind=kLoop, calls=%fused_computation.2 | loop fusion | flops 262144 | bytes 1048578 | tf_op jit(solution)/shard_map/jit(_where)/select_n | solution.py:264
  (17 shorter events, 0.2 us)
Async XLA Ops:
  0.0 1.0 %copy-start.5 = (bf16[512,2,128]{2,1,0:T(2,128)(2,1)S(1)}, bf16[512,2,128]{2,1,0:T(2,128)(2,1)}, u32[]{:S(2)}) copy-start(bf16[512,2,128]{2,1,0:T(2,128)(2,1)} %param.19) | copy-start | bytes 786436
  1.0 5.8 %copy-start.1 = (bf16[4,1024,64]{1,2,0:T(8,128)(2,1)S(1)}, bf16[4,1024,64]{1,2,0:T(8,128)(2,1)}, u32[]{:S(2)}) copy-start(bf16[4,1024,64]{1,2,0:T(8,128)(2,1)} %param.13) | copy-start | bytes 1572868
  1.1 5.8 %copy-start = (bf16[256,1024]{1,0:T(8,128)(2,1)S(1)}, bf16[256,1024]{1,0:T(8,128)(2,1)}, u32[]{:S(2)}) copy-start(bf16[256,1024]{1,0:T(8,128)(2,1)} %features_ref.1) | copy-start | bytes 1572868
  1.1 5.7 %copy-start.2 = (s32[4]{0:T(128)S(1)}, s32[4]{0:T(128)}, u32[]{:S(2)}) copy-start(s32[4]{0:T(128)} %ids_ref.3) | copy-start | bytes 52
  1.2 5.7 %copy-start.3 = (s32[4]{0:T(128)S(1)}, s32[4]{0:T(128)}, u32[]{:S(2)}) copy-start(s32[4]{0:T(128)} %order_ref.1) | copy-start | bytes 52
  1.2 19.2 %collective-permute-start.1 = (bf16[1024,128]{1,0:T(8,128)(2,1)S(1)}, bf16[1024,128]{1,0:T(8,128)(2,1)S(1)}, u32[]{:S(2)}, u32[]{:S(2)}) collective-permute-start(bf16[1024,128]{1,0:T(8,128)(2,1)S(1)} %fusion.1.refs_1_), channel_id=1, source_target_pairs={{0,8},{4,12},{8,0},{12,4},{1,9},{5,13},{9,1},{13,5},{2,10},{6,14},... | collective-permute-start | bytes 786440 | tf_op jit(solution)/shard_map/ppermute | solution.py:190
  5.3 16.4 %collective-permute-start.2 = (bf16[1024,128]{1,0:T(8,128)(2,1)S(1)}, bf16[1024,128]{1,0:T(8,128)(2,1)S(1)}, u32[]{:S(2)}, u32[]{:S(2)}) collective-permute-start(bf16[1024,128]{1,0:T(8,128)(2,1)S(1)} %fusion.1.refs_1_), channel_id=1, source_target_pairs={{0,4},{4,0},{8,12},{12,8},{1,5},{5,1},{9,13},{13,9},{2,6},{6,2},{1... | collective-permute-start | bytes 786440 | tf_op jit(solution)/shard_map/ppermute | solution.py:190
  6.9 1.1 %copy-start.4 = (bf16[256,2,4,128]{3,2,1,0:T(4,128)(2,1)S(1)}, bf16[256,2,4,128]{3,2,1,0:T(4,128)(2,1)}, u32[]{:S(2)}) copy-start(bf16[256,2,4,128]{3,2,1,0:T(4,128)(2,1)} %param.11) | copy-start | bytes 1572868
  7.9 1.9 %collective-permute-start.3 = (f32[64,256]{1,0:T(8,128)S(1)}, f32[64,256]{1,0:T(8,128)S(1)}, u32[]{:S(2)}, u32[]{:S(2)}) collective-permute-start(f32[64,256]{1,0:T(8,128)S(1)} %get-tuple-element.27), channel_id=1, source_target_pairs={{0,1},{1,0},{2,3},{3,2},{4,5},{5,4},{6,7},{7,6},{8,9},{9,8},{10,11... | collective-permute-start | bytes 196616 | tf_op jit(solution)/shard_map/ppermute | solution.py:176
  8.0 3.4 %copy-start.7 = (bf16[256,2,128]{2,1,0:T(2,128)(2,1)S(1)}, bf16[256,2,128]{2,1,0:T(2,128)(2,1)}, u32[]{:S(2)}) copy-start(bf16[256,2,128]{2,1,0:T(2,128)(2,1)} %param.16) | copy-start | bytes 393220
  8.2 3.2 %copy-start.6 = (bf16[256,2,128]{2,1,0:T(2,128)(2,1)S(1)}, bf16[256,2,128]{2,1,0:T(2,128)(2,1)}, u32[]{:S(2)}) copy-start(bf16[256,2,128]{2,1,0:T(2,128)(2,1)} %param.17) | copy-start | bytes 393220
  8.3 16.0 %collective-permute-start = (bf16[1024,128]{1,0:T(8,128)(2,1)S(1)}, bf16[1024,128]{1,0:T(8,128)(2,1)S(1)}, u32[]{:S(2)}, u32[]{:S(2)}) collective-permute-start(bf16[1024,128]{1,0:T(8,128)(2,1)S(1)} %bitcast.28), channel_id=1, source_target_pairs={{0,16},{16,0},{1,17},{17,1},{2,18},{18,2},{3,19},{19,3},{4,20},{20... | collective-permute-start | bytes 786440 | tf_op jit(solution)/shard_map/ppermute | solution.py:216
  9.8 4.3 %collective-permute-start.4 = (f32[64,256]{1,0:T(8,128)S(1)}, f32[64,256]{1,0:T(8,128)S(1)}, u32[]{:S(2)}, u32[]{:S(2)}) collective-permute-start(f32[64,256]{1,0:T(8,128)S(1)} %add.24), channel_id=1, source_target_pairs={{0,2},{1,3},{2,0},{3,1},{4,6},{5,7},{6,4},{7,5},{8,10},{9,11},{10,... | collective-permute-start | bytes 196616 | tf_op jit(solution)/shard_map/ppermute | solution.py:176
  11.7 3.5 %copy-start.9 = (bf16[4,64,2,128]{3,2,1,0:T(2,128)(2,1)S(1)}, bf16[4,64,2,128]{3,2,1,0:T(2,128)(2,1)}, u32[]{:S(2)}) copy-start(bf16[4,64,2,128]{3,2,1,0:T(2,128)(2,1)} %param.14) | copy-start | bytes 393220
  11.7 3.4 %copy-start.8 = (bf16[4,64,2,128]{3,2,1,0:T(2,128)(2,1)S(1)}, bf16[4,64,2,128]{3,2,1,0:T(2,128)(2,1)}, u32[]{:S(2)}) copy-start(bf16[4,64,2,128]{3,2,1,0:T(2,128)(2,1)} %param.15) | copy-start | bytes 393220
  14.2 4.3 %collective-permute-start.5 = (f32[64,256]{1,0:T(8,128)S(1)}, f32[64,256]{1,0:T(8,128)S(1)}, u32[]{:S(2)}, u32[]{:S(2)}) collective-permute-start(f32[64,256]{1,0:T(8,128)S(1)} %add.25.first), channel_id=1, source_target_pairs={{0,16},{16,0},{1,17},{17,1},{2,18},{18,2},{3,19},{19,3},{4,20},{20... | collective-permute-start | bytes 196616 | tf_op jit(solution)/shard_map/ppermute | solution.py:176
  19.3 8.3 %collective-permute-start.6 = (bf16[512,128]{1,0:T(8,128)(2,1)S(1)}, bf16[512,128]{1,0:T(8,128)(2,1)S(1)}, u32[]{:S(2)}, u32[]{:S(2)}) collective-permute-start(bf16[512,128]{1,0:T(8,128)(2,1)S(1)} %expand.1.refs_4_), channel_id=1, source_target_pairs={{0,8},{4,12},{8,0},{12,4},{1,9},{5,13},{9,1},{13,5},{2,10},{6,14},... | collective-permute-start | bytes 393224 | tf_op jit(solution)/shard_map/ppermute | solution.py:190
  19.7 16.1 %collective-permute-start.8 = (bf16[512,128]{1,0:T(8,128)(2,1)S(1)}, bf16[512,128]{1,0:T(8,128)(2,1)S(1)}, u32[]{:S(2)}, u32[]{:S(2)}) collective-permute-start(bf16[512,128]{1,0:T(8,128)(2,1)S(1)} %expand.1.refs_4_), channel_id=1, source_target_pairs={{0,4},{4,0},{8,12},{12,8},{1,5},{5,1},{9,13},{13,9},{2,6},{6,2},{1... | collective-permute-start | bytes 393224 | tf_op jit(solution)/shard_map/ppermute | solution.py:190
  20.3 13.6 %collective-permute-start.7 = (bf16[1024,128]{1,0:T(8,128)(2,1)S(1)}, bf16[1024,128]{1,0:T(8,128)(2,1)S(1)}, u32[]{:S(2)}, u32[]{:S(2)}) collective-permute-start(bf16[1024,128]{1,0:T(8,128)(2,1)S(1)} %collective-permute-done.1.refs_2_), channel_id=1, source_target_pairs={{0,4},{4,0},{8,12},{12,8},{1,5},{5,1},{9,13},{13,9},{2,6},{6,2},{1... | collective-permute-start | bytes 786440 | tf_op jit(solution)/shard_map/ppermute | solution.py:190
  27.6 8.9 %collective-permute-start.9 = (bf16[512,128]{1,0:T(8,128)(2,1)S(1)}, bf16[512,128]{1,0:T(8,128)(2,1)S(1)}, u32[]{:S(2)}, u32[]{:S(2)}) collective-permute-start(bf16[512,128]{1,0:T(8,128)(2,1)S(1)} %collective-permute-done.6.refs_5_), channel_id=1, source_target_pairs={{0,4},{4,0},{8,12},{12,8},{1,5},{5,1},{9,13},{13,9},{2,6},{6,2},{1... | collective-permute-start | bytes 393224 | tf_op jit(solution)/shard_map/ppermute | solution.py:190
  37.2 6.4 %collective-permute-start.10 = (bf16[1024,128]{1,0:T(8,128)(2,1)S(1)}, bf16[1024,128]{1,0:T(8,128)(2,1)S(1)}, u32[]{:S(2)}, u32[]{:S(2)}) collective-permute-start(bf16[1024,128]{1,0:T(8,128)(2,1)S(1)} %attend.13), channel_id=1, source_target_pairs={{0,16},{16,0},{1,17},{17,1},{2,18},{18,2},{3,19},{19,3},{4,20},{20... | collective-permute-start | bytes 786440 | tf_op jit(solution)/shard_map/ppermute | solution.py:216

commit v3 on v2

--- a/solution.py
+++ b/solution.py
@@ -22,30 +22,31 @@
     return lax.dot_general(a, b, (((1,), (1,)), ((), ())), preferred_element_type=jnp.float32)
 
 
-def latent_kernel(ids_ref, order_ref, features_ref, down_ref, out_ref, bound_ref, held, sem):
+def latent_kernel(ids_ref, order_ref, features_ref, down_ref, out_ref, bound_ref, chosen_ref):
     me = lax.axis_index("blk")
-    copy = pltpu.make_async_copy(down_ref.at[ids_ref[me]], held, sem)
-    copy.start()
+    chosen = ids_ref[me]
+    out_ref[...] = dot_t(down_ref[chosen], features_ref[...])
     tokens = features_ref.shape[0]
+    lanes = (1, bound_ref.shape[1])
     for mask in range(order_ref.shape[0]):
         bound = (order_ref[me] - order_ref[me ^ mask]) * tokens
-        bound_ref[mask : mask + 1, :] = jnp.full((1, bound_ref.shape[1]), bound, jnp.int32)
-    copy.wait()
-    out_ref[...] = dot_t(held[...], features_ref[...])
+        bound_ref[mask : mask + 1, :] = jnp.full(lanes, bound, jnp.int32)
+    for adapter in range(down_ref.shape[0]):
+        chosen_ref[adapter : adapter + 1, :] = jnp.full(lanes, chosen - adapter, jnp.int32)
 
 
 def partial_latent(ids, order, features, down):
     tokens, depth = features.shape
-    rank = down.shape[1]
+    adapters, rank, _ = down.shape
     return pl.pallas_call(
         latent_kernel,
         out_shape=[
             jax.ShapeDtypeStruct((rank, tokens), jnp.float32),
             jax.ShapeDtypeStruct((order.shape[0], 128), jnp.int32),
+            jax.ShapeDtypeStruct((adapters, 128), jnp.int32),
         ],
-        in_specs=[SMEM, SMEM, VMEM, pl.BlockSpec(memory_space=pl.ANY)],
-        out_specs=[VMEM, VMEM],
-        scratch_shapes=[pltpu.VMEM((rank, depth), down.dtype), pltpu.SemaphoreType.DMA(())],
+        in_specs=[SMEM, SMEM, VMEM, VMEM],
+        out_specs=[VMEM] * 3,
         compiler_params=pltpu.CompilerParams(vmem_limit_bytes=LIMIT),
         cost_estimate=pl.CostEstimate(
             flops=2 * tokens * depth * rank,
@@ -56,25 +57,28 @@
     )(ids, order, features, down)
 
 
-def expand_kernel(ids_ref, first, second, key_up, value_up, key_base, value_base, out_ref):
-    chosen = ids_ref[lax.axis_index("blk")]
+def expand_kernel(chosen_ref, first, second, key_up, value_up, key_base, value_base, out_ref):
     latent = (first[...] + second[...]).astype(jnp.bfloat16)
     tokens = key_base.shape[0]
     for n, (up, base) in enumerate(((key_up, key_base), (value_up, value_base))):
-        delta = lax.dot_general(
-            latent, up[chosen], (((0,), (0,)), ((), ())), preferred_element_type=jnp.float32
-        )
+        delta = None
+        for adapter in range(up.shape[0]):
+            term = lax.dot_general(
+                latent, up[adapter], (((0,), (0,)), ((), ())), preferred_element_type=jnp.float32
+            )
+            here = chosen_ref[adapter : adapter + 1, : term.shape[1]] == 0
+            delta = term if delta is None else jnp.where(here, term, delta)
         out_ref[n * tokens : (n + 1) * tokens, :] = (
             base[...].astype(jnp.float32) + delta
         ).astype(jnp.bfloat16)
 
 
-def expand(ids, first, second, key_up, value_up, key_base, value_base):
+def expand(chosen, first, second, key_up, value_up, key_base, value_base):
     tokens, head_dim = key_base.shape
     return pl.pallas_call(
         expand_kernel,
         out_shape=jax.ShapeDtypeStruct((2 * tokens, head_dim), jnp.bfloat16),
-        in_specs=[SMEM] + [VMEM] * 6,
+        in_specs=[VMEM] * 7,
         out_specs=VMEM,
         compiler_params=pltpu.CompilerParams(vmem_limit_bytes=LIMIT),
         cost_estimate=pl.CostEstimate(
@@ -83,7 +87,32 @@
             transcendentals=0,
         ),
         name="expand",
-    )(ids, first, second, key_up, value_up, key_base, value_base)
+    )(chosen, first, second, key_up, value_up, key_base, value_base)
+
+
+def place_kernel(aliased, *refs):
+    part_ref, out_ref, sem = refs[-3:]
+    mine = lax.axis_index("team") & 1
+    head = 1 - mine if aliased else mine
+    copy = pltpu.make_async_copy(part_ref, out_ref.at[:, head], sem)
+    copy.start()
+    copy.wait()
+
+
+def place(part, result, heads):
+    tokens, group, head_dim = part.shape
+    whole = pl.BlockSpec(memory_space=pl.ANY)
+    operands = [part] if result is None else [result, part]
+    return pl.pallas_call(
+        functools.partial(place_kernel, result is not None),
+        out_shape=jax.ShapeDtypeStruct((tokens, heads, group, head_dim), part.dtype),
+        in_specs=[whole] * (len(operands) - 1) + [VMEM],
+        out_specs=whole,
+        scratch_shapes=[pltpu.SemaphoreType.DMA(())],
+        input_output_aliases={} if result is None else {0: 0},
+        compiler_params=pltpu.CompilerParams(vmem_limit_bytes=LIMIT),
+        name="place",
+    )(*operands)
 
 
 def wide(value, width):
@@ -207,7 +236,7 @@
 ):
     block_count = lax.axis_size("blk")
     team_count = lax.axis_size("team")
-    query_dev, _, group_dev, head_dim = queries.shape
+    query_dev, kv_heads, group_dev, head_dim = queries.shape
     mine = lax.axis_index("team") & 1
     scale = LOG2E / math.sqrt(head_dim)
     rows = query_dev * group_dev
@@ -219,7 +248,7 @@
         index = 1 - mine if other else mine
         return lax.dynamic_index_in_dim(array, index, axis, keepdims=False)
 
-    latent, bounds = partial_latent(adapter_ids, block_order, features, jnp.swapaxes(adapter_down, 1, 2))
+    latent, bounds, chosen = partial_latent(adapter_ids, block_order, features, jnp.swapaxes(adapter_down, 1, 2))
     own_prefix = pick(jnp.concatenate([prefix_key, prefix_value], axis=0), 1)
     first, second = butterfly(latent, "head", lax.axis_size("head"))
     first, second = butterfly(first + second, "team", team_count)
@@ -228,7 +257,7 @@
     own_queries = pick(queries, 1).reshape(rows, head_dim)
     far_queries = swap(pick(queries, 1, True).reshape(rows, head_dim))
     own_new = expand(
-        adapter_ids,
+        chosen,
         first,
         second,
         pick(adapter_key_up, 2),
@@ -258,10 +287,9 @@
         out = attend(bounds, far_queries, far_state, tail[-1:], True, group_dev, scale, span)[0]
         received.append(swap(out))
     own_out = attend(bounds, own_queries, own_state, relayed + tail, True, group_dev, scale)[0]
-    shape = (query_dev, 1, group_dev, head_dim)
-    head = lax.broadcasted_iota(jnp.int32, queries.shape, 1)
-    received = jnp.concatenate(received, axis=0)
-    return jnp.where(head == mine, own_out.reshape(shape), received.reshape(shape))
+    shape = (query_dev, group_dev, head_dim)
+    result = place(own_out.reshape(shape), None, kv_heads)
+    return place(received[0].reshape(shape), result, kv_heads)
 
 
 def solution(mesh):

time: 44.9 us -> 43.9 us (0.978)
  other arithmetic: 1.18 us -> 0.05 us
  Pallas kernels: 13 us -> 13.7 us
    pallas_call x0 -> x2, Pallas kernels: none -> 1.43 us  [place(): pl.pallas_call(functools.partial(place_kernel, result is not None), out_s...]
    select_n x1 -> x0, other arithmetic: 1.13 us -> none  [on_device(): jnp.where(head == mine, own_out.reshape(shape), received.reshape(shape))]
    ppermute x6, waiting for transfers between devices: 6.08 us -> 5.11 us  [gather_blocks(): held[mask ^ step] = lax.ppermute(sent, 'blk', perm)]
    ppermute x2, starting transfers between devices: 3.33 us -> 2.45 us  [swap(): return lax.ppermute(value, 'team', [(i, i ^ 1) for i in range(team_count)])]
    ppermute x6, starting transfers between devices: 8.13 us -> 8.96 us  [gather_blocks(): held[mask ^ step] = lax.ppermute(sent, 'blk', perm)]
  transfers between devices with their start and end apart: 11 -> 11, of which waited for: 5 -> 5; matrix products, arithmetic and copies ran while one was open for 2% -> 2% of each run, Pallas kernels for 27% -> 28%
where the time goes in v3:
time: 43.9 us; the launch traced here: 43.7 us
  waiting for transfers between devices  14 us (32%)
  starting transfers between devices  13.7 us (31%)
  Pallas kernels  13.7 us (31%)
  local copies, waits for them, and re-layouts  2.04 us (5%)
    pallas_call x7, Pallas kernels, attend(): pl.pallas_call(functools.partial(attend_kernel, span, masks, state is not...  11.1 us
    ppermute x6, starting transfers between devices, gather_blocks(): held[mask ^ step] = lax.ppermute(sent, 'blk', perm)  8.96 us
    ppermute x3, waiting for transfers between devices, butterfly(): pair = (value, lax.ppermute(value, axis, perm))  5.79 us
    ppermute x6, waiting for transfers between devices, gather_blocks(): held[mask ^ step] = lax.ppermute(sent, 'blk', perm)  5.11 us
    ppermute x2, waiting for transfers between devices, swap(): return lax.ppermute(value, 'team', [(i, i ^ 1) for i in range(team_count)])  3.1 us
    ppermute x2, starting transfers between devices, swap(): return lax.ppermute(value, 'team', [(i, i ^ 1) for i in range(team_count)])  2.45 us
    ppermute x3, starting transfers between devices, butterfly(): pair = (value, lax.ppermute(value, axis, perm))  2.26 us
    pallas_call x2, Pallas kernels, place(): pl.pallas_call(functools.partial(place_kernel, result is not None), out_s...  1.43 us
  transfers between devices with their start and end apart: 11, of which 5 were waited for; matrix products, arithmetic and copies ran while one was open for 2% of the time, Pallas kernels for 28%

profile of v3, /device:TPU:0, one launch (start us, length us, event | category | flops | bytes accessed | tf_op | source)
XLA Modules:
  0.0 43.7 jit_solution(1532420357518906249)
XLA Ops:
  0.0 1.0 %copy.13 = bf16[512,2,128]{2,0,1:T(8,128)(2,1)S(1)} copy(bf16[512,2,128]{2,1,0:T(2,128)(2,1)} %param.18) | data formatting | bytes 524288 | tf_op args[7]
  1.0 0.0 copy-start.1
  1.1 0.0 copy-start
  1.1 0.0 copy-start.2
  1.2 0.0 copy-start.3
  1.2 4.1 %collective-permute-start.1 = (bf16[1024,128]{1,0:T(8,128)(2,1)S(1)}, bf16[1024,128]{1,0:T(8,128)(2,1)S(1)}, u32[]{:S(2)}, u32[]{:S(2)}) collective-permute-start(bf16[1024,128]{1,0:T(8,128)(2,1)S(1)} %fusion.1.refs_1_), channel_id=1, source_target_pairs={{0,8},{4,12},{8,0},{12,4},{1,9},{5,13},{9,1},{13,5},{2,10},{6,14},... | collective-permute-start | bytes 786440 | tf_op jit(solution)/shard_map/ppermute | solution.py:219
  5.3 0.0 copy-done.1
  5.3 0.0 copy-start.4
  5.3 0.8 %partial_latent.1 = (f32[64,256]{1,0:T(8,128)S(1)}, s32[4,128]{1,0:T(4,128)S(1)}, s32[4,128]{1,0:T(4,128)S(1)}) custom-call(s32[4]{0:T(128)S(1)} %copy-done.2, s32[4]{0:T(128)S(1)} %copy-done.3, bf16[256,1024]{1,0:T(8,128)(2,1)S(1)} %copy-done, bf16[4,64,1024]{2,1,0:T(8,128)(2,1)S(1)} %bitcast.22), custom_call_target="tpu_custom_call" | custom-call | flops 33554432 | bytes 655360 | tf_op jit(solution)/shard_map/partial_latent/pallas_call | solution.py:41
  6.2 0.1 collective-permute-start.3
  6.2 0.1 copy-done.4
  6.4 0.2 constant_dynamic-slice_fusion.4
  6.5 0.0 copy-start.6
  6.6 1.6 %collective-permute-start = (bf16[1024,128]{1,0:T(8,128)(2,1)S(1)}, bf16[1024,128]{1,0:T(8,128)(2,1)S(1)}, u32[]{:S(2)}, u32[]{:S(2)}) collective-permute-start(bf16[1024,128]{1,0:T(8,128)(2,1)S(1)} %bitcast.29), channel_id=1, source_target_pairs={{0,16},{16,0},{1,17},{17,1},{2,18},{18,2},{3,19},{19,3},{4,20},{20... | collective-permute-start | bytes 786440 | tf_op jit(solution)/shard_map/ppermute | solution.py:245
  8.1 1.6 %collective-permute-start.2 = (bf16[1024,128]{1,0:T(8,128)(2,1)S(1)}, bf16[1024,128]{1,0:T(8,128)(2,1)S(1)}, u32[]{:S(2)}, u32[]{:S(2)}) collective-permute-start(bf16[1024,128]{1,0:T(8,128)(2,1)S(1)} %fusion.1.refs_1_), channel_id=1, source_target_pairs={{0,4},{4,0},{8,12},{12,8},{1,5},{5,1},{9,13},{13,9},{2,6},{6,2},{1... | collective-permute-start | bytes 786440 | tf_op jit(solution)/shard_map/ppermute | solution.py:219
  9.7 0.0 collective-permute-done.3
  9.7 1.6 %collective-permute-start.4 = (f32[64,256]{1,0:T(8,128)S(1)}, f32[64,256]{1,0:T(8,128)S(1)}, u32[]{:S(2)}, u32[]{:S(2)}) collective-permute-start(f32[64,256]{1,0:T(8,128)S(1)} %add.24), channel_id=1, source_target_pairs={{0,2},{1,3},{2,0},{3,1},{4,6},{5,7},{6,4},{7,5},{8,10},{9,11},{10,... | collective-permute-start | bytes 196616 | tf_op jit(solution)/shard_map/ppermute | solution.py:205
  11.3 0.0 copy-done.7
  11.3 0.3 constant_dynamic-slice_fusion.2
  11.6 0.0 copy-start.9
  11.7 0.0 copy-start.8
  11.7 2.4 %collective-permute-done.4 = f32[64,256]{1,0:T(8,128)S(1)} collective-permute-done((f32[64,256]{1,0:T(8,128)S(1)}, f32[64,256]{1,0:T(8,128)S(1)}, u32[]{:S(2)}, u32[]{:S(2)}) %collective-permute-start.4) | collective-permute-done | bytes 65568 | tf_op jit(solution)/shard_map/ppermute | solution.py:205
  14.1 0.6 %collective-permute-start.5 = (f32[64,256]{1,0:T(8,128)S(1)}, f32[64,256]{1,0:T(8,128)S(1)}, u32[]{:S(2)}, u32[]{:S(2)}) collective-permute-start(f32[64,256]{1,0:T(8,128)S(1)} %add.25.first), channel_id=1, source_target_pairs={{0,16},{16,0},{1,17},{17,1},{2,18},{18,2},{3,19},{19,3},{4,20},{20... | collective-permute-start | bytes 196616 | tf_op jit(solution)/shard_map/ppermute | solution.py:205
  14.7 0.3 constant_dynamic-slice_fusion
  15.0 3.4 %collective-permute-done.5.second = f32[64,256]{1,0:T(8,128)S(1)} collective-permute-done((f32[64,256]{1,0:T(8,128)S(1)}, f32[64,256]{1,0:T(8,128)S(1)}, u32[]{:S(2)}, u32[]{:S(2)}) %collective-permute-start.5) | collective-permute-done | bytes 65568 | tf_op jit(solution)/shard_map/ppermute | solution.py:205
  18.4 0.3 expand.1.refs_4_
  18.7 1.1 %collective-permute-start.6 = (bf16[512,128]{1,0:T(8,128)(2,1)S(1)}, bf16[512,128]{1,0:T(8,128)(2,1)S(1)}, u32[]{:S(2)}, u32[]{:S(2)}) collective-permute-start(bf16[512,128]{1,0:T(8,128)(2,1)S(1)} %expand.1.refs_4_), channel_id=1, source_target_pairs={{0,8},{4,12},{8,0},{12,4},{1,9},{5,13},{9,1},{13,5},{2,10},{6,14},... | collective-permute-start | bytes 393224 | tf_op jit(solution)/shard_map/ppermute | solution.py:219
  19.8 0.5 %collective-permute-start.8 = (bf16[512,128]{1,0:T(8,128)(2,1)S(1)}, bf16[512,128]{1,0:T(8,128)(2,1)S(1)}, u32[]{:S(2)}, u32[]{:S(2)}) collective-permute-start(bf16[512,128]{1,0:T(8,128)(2,1)S(1)} %expand.1.refs_4_), channel_id=1, source_target_pairs={{0,4},{4,0},{8,12},{12,8},{1,5},{5,1},{9,13},{13,9},{2,6},{6,2},{1... | collective-permute-start | bytes 393224 | tf_op jit(solution)/shard_map/ppermute | solution.py:219
  20.2 0.0 collective-permute-done.1.refs_2_
  20.3 1.6 %collective-permute-start.7 = (bf16[1024,128]{1,0:T(8,128)(2,1)S(1)}, bf16[1024,128]{1,0:T(8,128)(2,1)S(1)}, u32[]{:S(2)}, u32[]{:S(2)}) collective-permute-start(bf16[1024,128]{1,0:T(8,128)(2,1)S(1)} %collective-permute-done.1.refs_2_), channel_id=1, source_target_pairs={{0,4},{4,0},{8,12},{12,8},{1,5},{5,1},{9,13},{13,9},{2,6},{6,2},{1... | collective-permute-start | bytes 786440 | tf_op jit(solution)/shard_map/ppermute | solution.py:219
  21.8 0.0 collective-permute-done.refs_0_.refs_1_
  21.8 0.4 collective-permute-done.2.refs_3_
  22.2 2.4 %attend.7 = (f32[1024,128]{1,0:T(8,128)S(1)}, f32[1024,256]{1,0:T(8,128)S(1)}) custom-call(bf16[1024,128]{1,0:T(8,128)(2,1)S(1)} %collective-permute-done.refs_0_.refs_1_, bf16[1024,128]{1,0:T(8,128)(2,1)S(1)} %fusion.1.refs_1_, bf16[1024,128]{1,0:T(8,128)(2,1)S(1)} %collective-permute-done.1.refs_2_, bf16[1024,128]{1,0:T(8,128)(2,1)S(1)} %collective-permute-done.2.refs_3_), custom_call_target="tpu_custom_call" | custom-call | flops 1207959552 | bytes 524288 | tf_op jit(solution)/shard_map/attend/pallas_call | solution.py:184
  24.6 2.4 %attend.9 = (f32[1024,128]{1,0:T(8,128)S(1)}, f32[1024,256]{1,0:T(8,128)S(1)}) custom-call(bf16[1024,128]{1,0:T(8,128)(2,1)S(1)} %bitcast.19, bf16[1024,128]{1,0:T(8,128)(2,1)S(1)} %fusion.1.refs_1_, bf16[1024,128]{1,0:T(8,128)(2,1)S(1)} %collective-permute-done.1.refs_2_, bf16[1024,128]{1,0:T(8,128)(2,1)S(1)} %collective-permute-done.2.refs_3_), custom_call_target="tpu_custom_call" | custom-call | flops 1207959552 | bytes 524288 | tf_op jit(solution)/shard_map/attend/pallas_call | solution.py:184
  27.1 0.0 collective-permute-done.6.refs_5_
  27.1 0.2 collective-permute-start.9
  27.3 1.1 %attend.10 = (f32[1024,128]{1,0:T(8,128)S(1)}, f32[1024,256]{1,0:T(8,128)S(1)}) custom-call(s32[4,128]{1,0:T(4,128)S(1)} %get-tuple-element.25.refs_0_, bf16[1024,128]{1,0:T(8,128)(2,1)S(1)} %bitcast.20, f32[1024,128]{1,0:T(8,128)S(1)} %get-tuple-element.34.refs_2_, f32[1024,256]{1,0:T(8,128)S(1)} %get-tuple-element.35.refs_3_, ...), custom_call_target="tpu_custom_call" | custom-call | flops 402653184 | bytes 524288 | tf_op jit(solution)/shard_map/attend/pallas_call | solution.py:184
  28.4 4.7 %collective-permute-done.7.refs_6_.refs_4_ = bf16[1024,128]{1,0:T(8,128)(2,1)S(1)} collective-permute-done((bf16[1024,128]{1,0:T(8,128)(2,1)S(1)}, bf16[1024,128]{1,0:T(8,128)(2,1)S(1)}, u32[]{:S(2)}, u32[]{:S(2)}) %collective-permute-start.7) | collective-permute-done | bytes 262176 | tf_op jit(solution)/shard_map/ppermute | solution.py:219
  33.1 1.8 %attend.8 = (f32[1024,128]{1,0:T(8,128)S(1)}, f32[1024,256]{1,0:T(8,128)S(1)}) custom-call(s32[4,128]{1,0:T(4,128)S(1)} %get-tuple-element.25.refs_0_, bf16[1024,128]{1,0:T(8,128)(2,1)S(1)} %collective-permute-done.refs_0_.refs_1_, f32[1024,128]{1,0:T(8,128)S(1)} %get-tuple-element.26.refs_2_, f32[1024,256]{1,0:T(8,128)S(1)} %get-tuple-element.27.refs_3_, ...), custom_call_target="tpu_custom_call" | custom-call | flops 805306368 | bytes 524288 | tf_op jit(solution)/shard_map/attend/pallas_call | solution.py:184
  35.0 0.0 collective-permute-done.8.refs_5_.refs_4_
  35.0 0.7 %attend.12 = (f32[1024,128]{1,0:T(8,128)S(1)}, f32[1024,256]{1,0:T(8,128)S(1)}) custom-call(s32[4,128]{1,0:T(4,128)S(1)} %get-tuple-element.25.refs_0_, bf16[1024,128]{1,0:T(8,128)(2,1)S(1)} %collective-permute-done.refs_0_.refs_1_, f32[1024,128]{1,0:T(8,128)S(1)} %get-tuple-element.41.refs_2_, f32[1024,256]{1,0:T(8,128)S(1)} %get-tuple-element.42.refs_3_, ...), custom_call_target="tpu_custom_call" | custom-call | flops 201326592 | bytes 524288 | tf_op jit(solution)/shard_map/attend/pallas_call | solution.py:184
  35.7 0.0 collective-permute-done.9.refs_6_.refs_4_
  35.7 0.7 %attend.13 = bf16[1024,128]{1,0:T(8,128)(2,1)S(1)} custom-call(s32[4,128]{1,0:T(4,128)S(1)} %get-tuple-element.25.refs_0_, bf16[1024,128]{1,0:T(8,128)(2,1)S(1)} %collective-permute-done.refs_0_.refs_1_, f32[1024,128]{1,0:T(8,128)S(1)} %get-tuple-element.43.refs_2_, f32[1024,256]{1,0:T(8,128)S(1)} %get-tuple-element.44.refs_3_, ...), custom_call_target="tpu_custom_call" | custom-call | flops 201326592 | bytes 524288 | tf_op jit(solution)/shard_map/attend/pallas_call | solution.py:184
  36.4 0.9 %collective-permute-start.10 = (bf16[1024,128]{1,0:T(8,128)(2,1)S(1)}, bf16[1024,128]{1,0:T(8,128)(2,1)S(1)}, u32[]{:S(2)}, u32[]{:S(2)}) collective-permute-start(bf16[1024,128]{1,0:T(8,128)(2,1)S(1)} %attend.13), channel_id=1, source_target_pairs={{0,16},{16,0},{1,17},{17,1},{2,18},{18,2},{3,19},{19,3},{4,20},{20... | collective-permute-start | bytes 786440 | tf_op jit(solution)/shard_map/ppermute | solution.py:245
  37.3 1.8 %attend.11 = bf16[1024,128]{1,0:T(8,128)(2,1)S(1)} custom-call(s32[4,128]{1,0:T(4,128)S(1)} %get-tuple-element.25.refs_0_, bf16[1024,128]{1,0:T(8,128)(2,1)S(1)} %bitcast.21, f32[1024,128]{1,0:T(8,128)S(1)} %get-tuple-element.38.refs_2_, f32[1024,256]{1,0:T(8,128)S(1)} %get-tuple-element.39.refs_3_, ...), custom_call_target="tpu_custom_call" | custom-call | flops 805306368 | bytes 524288 | tf_op jit(solution)/shard_map/attend/pallas_call | solution.py:184
  39.2 0.7 %place.2.refs_0_ = bf16[256,2,4,128]{3,2,1,0:T(4,128)(2,1)} custom-call(bf16[256,4,128]{2,1,0:T(4,128)(2,1)S(1)} %bitcast.24), custom_call_target="tpu_custom_call" | custom-call | tf_op jit(solution)/shard_map/place/pallas_call | solution.py:106
  39.9 3.1 %collective-permute-done.10 = bf16[1024,128]{1,0:T(8,128)(2,1)S(1)} collective-permute-done((bf16[1024,128]{1,0:T(8,128)(2,1)S(1)}, bf16[1024,128]{1,0:T(8,128)(2,1)S(1)}, u32[]{:S(2)}, u32[]{:S(2)}) %collective-permute-start.10) | collective-permute-done | bytes 262176 | tf_op jit(solution)/shard_map/ppermute | solution.py:245
  43.0 0.7 %place.3 = bf16[256,2,4,128]{3,2,1,0:T(4,128)(2,1)} custom-call(bf16[256,2,4,128]{3,2,1,0:T(4,128)(2,1)} %place.2.refs_0_, bf16[256,4,128]{2,1,0:T(4,128)(2,1)S(1)} %bitcast.23), custom_call_target="tpu_custom_call", output_to_operand_aliasing={{}: (0, {})} | custom-call | tf_op jit(solution)/shard_map/place/pallas_call | solution.py:106
  (17 shorter events, 0.1 us)
Async XLA Ops:
  0.0 1.0 %copy-start.5 = (bf16[512,2,128]{2,1,0:T(2,128)(2,1)S(1)}, bf16[512,2,128]{2,1,0:T(2,128)(2,1)}, u32[]{:S(2)}) copy-start(bf16[512,2,128]{2,1,0:T(2,128)(2,1)} %param.19) | copy-start | bytes 786436
  1.0 4.3 %copy-start.1 = (bf16[4,1024,64]{1,2,0:T(8,128)(2,1)S(1)}, bf16[4,1024,64]{1,2,0:T(8,128)(2,1)}, u32[]{:S(2)}) copy-start(bf16[4,1024,64]{1,2,0:T(8,128)(2,1)} %param.13) | copy-start | bytes 1572868
  1.1 4.2 %copy-start = (bf16[256,1024]{1,0:T(8,128)(2,1)S(1)}, bf16[256,1024]{1,0:T(8,128)(2,1)}, u32[]{:S(2)}) copy-start(bf16[256,1024]{1,0:T(8,128)(2,1)} %features_ref.1) | copy-start | bytes 1572868
  1.1 4.2 %copy-start.2 = (s32[4]{0:T(128)S(1)}, s32[4]{0:T(128)}, u32[]{:S(2)}) copy-start(s32[4]{0:T(128)} %ids_ref.1) | copy-start | bytes 52
  1.2 4.2 %copy-start.3 = (s32[4]{0:T(128)S(1)}, s32[4]{0:T(128)}, u32[]{:S(2)}) copy-start(s32[4]{0:T(128)} %order_ref.1) | copy-start | bytes 52
  1.2 19.1 %collective-permute-start.1 = (bf16[1024,128]{1,0:T(8,128)(2,1)S(1)}, bf16[1024,128]{1,0:T(8,128)(2,1)S(1)}, u32[]{:S(2)}, u32[]{:S(2)}) collective-permute-start(bf16[1024,128]{1,0:T(8,128)(2,1)S(1)} %fusion.1.refs_1_), channel_id=1, source_target_pairs={{0,8},{4,12},{8,0},{12,4},{1,9},{5,13},{9,1},{13,5},{2,10},{6,14},... | collective-permute-start | bytes 786440 | tf_op jit(solution)/shard_map/ppermute | solution.py:219
  5.3 1.0 %copy-start.4 = (bf16[256,2,4,128]{3,2,1,0:T(4,128)(2,1)S(1)}, bf16[256,2,4,128]{3,2,1,0:T(4,128)(2,1)}, u32[]{:S(2)}) copy-start(bf16[256,2,4,128]{3,2,1,0:T(4,128)(2,1)} %param.11) | copy-start | bytes 1572868
  6.2 3.5 %collective-permute-start.3 = (f32[64,256]{1,0:T(8,128)S(1)}, f32[64,256]{1,0:T(8,128)S(1)}, u32[]{:S(2)}, u32[]{:S(2)}) collective-permute-start(f32[64,256]{1,0:T(8,128)S(1)} %get-tuple-element.29), channel_id=1, source_target_pairs={{0,1},{1,0},{2,3},{3,2},{4,5},{5,4},{6,7},{7,6},{8,9},{9,8},{10,11... | collective-permute-start | bytes 196616 | tf_op jit(solution)/shard_map/ppermute | solution.py:205
  6.4 4.9 %copy-start.7 = (bf16[4,64,2,128]{3,2,1,0:T(2,128)(2,1)S(1)}, bf16[4,64,2,128]{3,2,1,0:T(2,128)(2,1)}, u32[]{:S(2)}) copy-start(bf16[4,64,2,128]{3,2,1,0:T(2,128)(2,1)} %param.14) | copy-start | bytes 393220
  6.5 4.8 %copy-start.6 = (bf16[4,64,2,128]{3,2,1,0:T(2,128)(2,1)S(1)}, bf16[4,64,2,128]{3,2,1,0:T(2,128)(2,1)}, u32[]{:S(2)}) copy-start(bf16[4,64,2,128]{3,2,1,0:T(2,128)(2,1)} %param.15) | copy-start | bytes 393220
  6.6 15.3 %collective-permute-start = (bf16[1024,128]{1,0:T(8,128)(2,1)S(1)}, bf16[1024,128]{1,0:T(8,128)(2,1)S(1)}, u32[]{:S(2)}, u32[]{:S(2)}) collective-permute-start(bf16[1024,128]{1,0:T(8,128)(2,1)S(1)} %bitcast.29), channel_id=1, source_target_pairs={{0,16},{16,0},{1,17},{17,1},{2,18},{18,2},{3,19},{19,3},{4,20},{20... | collective-permute-start | bytes 786440 | tf_op jit(solution)/shard_map/ppermute | solution.py:245
  8.1 14.1 %collective-permute-start.2 = (bf16[1024,128]{1,0:T(8,128)(2,1)S(1)}, bf16[1024,128]{1,0:T(8,128)(2,1)S(1)}, u32[]{:S(2)}, u32[]{:S(2)}) collective-permute-start(bf16[1024,128]{1,0:T(8,128)(2,1)S(1)} %fusion.1.refs_1_), channel_id=1, source_target_pairs={{0,4},{4,0},{8,12},{12,8},{1,5},{5,1},{9,13},{13,9},{2,6},{6,2},{1... | collective-permute-start | bytes 786440 | tf_op jit(solution)/shard_map/ppermute | solution.py:219
  9.7 4.3 %collective-permute-start.4 = (f32[64,256]{1,0:T(8,128)S(1)}, f32[64,256]{1,0:T(8,128)S(1)}, u32[]{:S(2)}, u32[]{:S(2)}) collective-permute-start(f32[64,256]{1,0:T(8,128)S(1)} %add.24), channel_id=1, source_target_pairs={{0,2},{1,3},{2,0},{3,1},{4,6},{5,7},{6,4},{7,5},{8,10},{9,11},{10,... | collective-permute-start | bytes 196616 | tf_op jit(solution)/shard_map/ppermute | solution.py:205
  11.6 3.0 %copy-start.9 = (bf16[256,2,128]{2,1,0:T(2,128)(2,1)S(1)}, bf16[256,2,128]{2,1,0:T(2,128)(2,1)}, u32[]{:S(2)}) copy-start(bf16[256,2,128]{2,1,0:T(2,128)(2,1)} %param.16) | copy-start | bytes 393220
  11.7 3.0 %copy-start.8 = (bf16[256,2,128]{2,1,0:T(2,128)(2,1)S(1)}, bf16[256,2,128]{2,1,0:T(2,128)(2,1)}, u32[]{:S(2)}) copy-start(bf16[256,2,128]{2,1,0:T(2,128)(2,1)} %param.17) | copy-start | bytes 393220
  14.1 4.3 %collective-permute-start.5 = (f32[64,256]{1,0:T(8,128)S(1)}, f32[64,256]{1,0:T(8,128)S(1)}, u32[]{:S(2)}, u32[]{:S(2)}) collective-permute-start(f32[64,256]{1,0:T(8,128)S(1)} %add.25.first), channel_id=1, source_target_pairs={{0,16},{16,0},{1,17},{17,1},{2,18},{18,2},{3,19},{19,3},{4,20},{20... | collective-permute-start | bytes 196616 | tf_op jit(solution)/shard_map/ppermute | solution.py:205
  18.7 8.4 %collective-permute-start.6 = (bf16[512,128]{1,0:T(8,128)(2,1)S(1)}, bf16[512,128]{1,0:T(8,128)(2,1)S(1)}, u32[]{:S(2)}, u32[]{:S(2)}) collective-permute-start(bf16[512,128]{1,0:T(8,128)(2,1)S(1)} %expand.1.refs_4_), channel_id=1, source_target_pairs={{0,8},{4,12},{8,0},{12,4},{1,9},{5,13},{9,1},{13,5},{2,10},{6,14},... | collective-permute-start | bytes 393224 | tf_op jit(solution)/shard_map/ppermute | solution.py:219
  19.8 15.2 %collective-permute-start.8 = (bf16[512,128]{1,0:T(8,128)(2,1)S(1)}, bf16[512,128]{1,0:T(8,128)(2,1)S(1)}, u32[]{:S(2)}, u32[]{:S(2)}) collective-permute-start(bf16[512,128]{1,0:T(8,128)(2,1)S(1)} %expand.1.refs_4_), channel_id=1, source_target_pairs={{0,4},{4,0},{8,12},{12,8},{1,5},{5,1},{9,13},{13,9},{2,6},{6,2},{1... | collective-permute-start | bytes 393224 | tf_op jit(solution)/shard_map/ppermute | solution.py:219
  20.3 12.9 %collective-permute-start.7 = (bf16[1024,128]{1,0:T(8,128)(2,1)S(1)}, bf16[1024,128]{1,0:T(8,128)(2,1)S(1)}, u32[]{:S(2)}, u32[]{:S(2)}) collective-permute-start(bf16[1024,128]{1,0:T(8,128)(2,1)S(1)} %collective-permute-done.1.refs_2_), channel_id=1, source_target_pairs={{0,4},{4,0},{8,12},{12,8},{1,5},{5,1},{9,13},{13,9},{2,6},{6,2},{1... | collective-permute-start | bytes 786440 | tf_op jit(solution)/shard_map/ppermute | solution.py:219
  27.1 8.6 %collective-permute-start.9 = (bf16[512,128]{1,0:T(8,128)(2,1)S(1)}, bf16[512,128]{1,0:T(8,128)(2,1)S(1)}, u32[]{:S(2)}, u32[]{:S(2)}) collective-permute-start(bf16[512,128]{1,0:T(8,128)(2,1)S(1)} %collective-permute-done.6.refs_5_), channel_id=1, source_target_pairs={{0,4},{4,0},{8,12},{12,8},{1,5},{5,1},{9,13},{13,9},{2,6},{6,2},{1... | collective-permute-start | bytes 393224 | tf_op jit(solution)/shard_map/ppermute | solution.py:219
  36.4 6.6 %collective-permute-start.10 = (bf16[1024,128]{1,0:T(8,128)(2,1)S(1)}, bf16[1024,128]{1,0:T(8,128)(2,1)S(1)}, u32[]{:S(2)}, u32[]{:S(2)}) collective-permute-start(bf16[1024,128]{1,0:T(8,128)(2,1)S(1)} %attend.13), channel_id=1, source_target_pairs={{0,16},{16,0},{1,17},{17,1},{2,18},{18,2},{3,19},{19,3},{4,20},{20... | collective-permute-start | bytes 786440 | tf_op jit(solution)/shard_map/ppermute | solution.py:245

commit v4 on v3

--- a/solution.py
+++ b/solution.py
@@ -196,15 +196,16 @@
     )(*table, *operands)
 
 
-def butterfly(value, axis, size):
-    step = 1
-    pair = (value, None)
-    while step < size:
-        value = pair[0] if pair[1] is None else pair[0] + pair[1]
-        perm = [(i, i ^ step) for i in range(size)]
-        pair = (value, lax.ppermute(value, axis, perm))
-        step *= 2
-    return pair
+def latent_pair(value):
+    heads, teams = lax.axis_size("head"), lax.axis_size("team")
+    steps = [("head", 1 << n) for n in range(heads.bit_length() - 1)]
+    steps[1:1] = [("team", 1 << n) for n in range(teams.bit_length() - 1)]
+    received = None
+    for axis, step in steps:
+        value = value if received is None else value + received
+        perm = [(i, i ^ step) for i in range(lax.axis_size(axis))]
+        received = lax.ppermute(value, axis, perm)
+    return value, received
 
 
 def gather_blocks(value, count, before=None):
@@ -250,9 +251,7 @@
 
     latent, bounds, chosen = partial_latent(adapter_ids, block_order, features, jnp.swapaxes(adapter_down, 1, 2))
     own_prefix = pick(jnp.concatenate([prefix_key, prefix_value], axis=0), 1)
-    first, second = butterfly(latent, "head", lax.axis_size("head"))
-    first, second = butterfly(first + second, "team", team_count)
-
+    first, second = latent_pair(latent)
     prefix, _ = gather_blocks(own_prefix, block_count)
     own_queries = pick(queries, 1).reshape(rows, head_dim)
     far_queries = swap(pick(queries, 1, True).reshape(rows, head_dim))
@@ -274,7 +273,6 @@
     relayed = [(None, prefix[last])]
     middle = [(mask, new[mask]) for mask in new if mask in (0, half)]
     tail = [(mask, new[mask]) for mask in new if mask not in (0, half)]
-    own_state = attend(bounds, own_queries, own_state, middle, False, group_dev, scale)
     far_state = attend(bounds, far_queries, far_state, middle + relayed, False, group_dev, scale)
     far_state, own_state = lax.optimization_barrier((far_state, own_state))
     near = [(mask, piece) for mask, piece in tail if mask != last]
@@ -286,7 +284,7 @@
         span = (n * part, part)
         out = attend(bounds, far_queries, far_state, tail[-1:], True, group_dev, scale, span)[0]
         received.append(swap(out))
-    own_out = attend(bounds, own_queries, own_state, relayed + tail, True, group_dev, scale)[0]
+    own_out = attend(bounds, own_queries, own_state, relayed + middle + tail, True, group_dev, scale)[0]
     shape = (query_dev, group_dev, head_dim)
     result = place(own_out.reshape(shape), None, kv_heads)
     return place(received[0].reshape(shape), result, kv_heads)

time: 43.9 us -> 45.2 us (1.030)
  starting transfers between devices: 13.7 us -> 14.9 us
    ppermute x3, waiting for transfers between devices: 5.79 us -> 9.18 us  [latent_pair(): received = lax.ppermute(value, axis, perm)]
    ppermute x2, waiting for transfers between devices: 3.1 us -> 1.44 us  [swap(): return lax.ppermute(value, 'team', [(i, i ^ 1) for i in range(team_count)])]
    ppermute x6, waiting for transfers between devices: 5.11 us -> 3.58 us  [gather_blocks(): held[mask ^ step] = lax.ppermute(sent, 'blk', perm)]
    ppermute x2, starting transfers between devices: 2.45 us -> 3.11 us  [swap(): return lax.ppermute(value, 'team', [(i, i ^ 1) for i in range(team_count)])]
    pallas_call x7 -> x6, Pallas kernels: 11.1 us -> 11 us  [attend(): pl.pallas_call(functools.partial(attend_kernel, span, masks, state is not...]
  transfers between devices with their start and end apart: 11 -> 11, of which waited for: 5 -> 4; matrix products, arithmetic and copies ran while one was open for 2% -> 2% of each run, Pallas kernels for 28% -> 27%
where the time goes in v4:
time: 45.2 us; the launch traced here: 45 us
  starting transfers between devices  14.9 us (33%)
  waiting for transfers between devices  14.2 us (31%)
  Pallas kernels  13.5 us (30%)
  local copies, waits for them, and re-layouts  2.04 us (5%)
    pallas_call x6, Pallas kernels, attend(): pl.pallas_call(functools.partial(attend_kernel, span, masks, state is not...  11 us
    ppermute x6, starting transfers between devices, gather_blocks(): held[mask ^ step] = lax.ppermute(sent, 'blk', perm)  9.23 us
    ppermute x3, waiting for transfers between devices, latent_pair(): received = lax.ppermute(value, axis, perm)  9.18 us
    ppermute x6, waiting for transfers between devices, gather_blocks(): held[mask ^ step] = lax.ppermute(sent, 'blk', perm)  3.58 us
    ppermute x2, starting transfers between devices, swap(): return lax.ppermute(value, 'team', [(i, i ^ 1) for i in range(team_count)])  3.11 us
    ppermute x3, starting transfers between devices, latent_pair(): received = lax.ppermute(value, axis, perm)  2.56 us
    ppermute x2, waiting for transfers between devices, swap(): return lax.ppermute(value, 'team', [(i, i ^ 1) for i in range(team_count)])  1.44 us
    pallas_call x2, Pallas kernels, place(): pl.pallas_call(functools.partial(place_kernel, result is not None), out_s...  1.43 us
  transfers between devices with their start and end apart: 11, of which 4 were waited for; matrix products, arithmetic and copies ran while one was open for 2% of the time, Pallas kernels for 27%

profile of v4, /device:TPU:0, one launch (start us, length us, event | category | flops | bytes accessed | tf_op | source)
XLA Modules:
  0.0 45.0 jit_solution(17227207978063482484)
XLA Ops:
  0.0 1.0 %copy.13 = bf16[512,2,128]{2,0,1:T(8,128)(2,1)S(1)} copy(bf16[512,2,128]{2,1,0:T(2,128)(2,1)} %param.18) | data formatting | bytes 524288 | tf_op args[7]
  1.0 0.0 copy-done.5
  1.0 0.0 copy-start.1
  1.1 0.0 copy-start
  1.1 0.0 copy-start.2
  1.2 0.0 copy-start.3
  1.2 4.1 %collective-permute-start.1 = (bf16[1024,128]{1,0:T(8,128)(2,1)S(1)}, bf16[1024,128]{1,0:T(8,128)(2,1)S(1)}, u32[]{:S(2)}, u32[]{:S(2)}) collective-permute-start(bf16[1024,128]{1,0:T(8,128)(2,1)S(1)} %fusion.1.refs_1_), channel_id=1, source_target_pairs={{0,8},{4,12},{8,0},{12,4},{1,9},{5,13},{9,1},{13,5},{2,10},{6,14},... | collective-permute-start | bytes 786440 | tf_op jit(solution)/shard_map/ppermute | solution.py:220
  5.3 1.6 %collective-permute-start.2 = (bf16[1024,128]{1,0:T(8,128)(2,1)S(1)}, bf16[1024,128]{1,0:T(8,128)(2,1)S(1)}, u32[]{:S(2)}, u32[]{:S(2)}) collective-permute-start(bf16[1024,128]{1,0:T(8,128)(2,1)S(1)} %fusion.1.refs_1_), channel_id=1, source_target_pairs={{0,4},{4,0},{8,12},{12,8},{1,5},{5,1},{9,13},{13,9},{2,6},{6,2},{1... | collective-permute-start | bytes 786440 | tf_op jit(solution)/shard_map/ppermute | solution.py:220
  6.9 0.0 copy-done.1
  6.9 0.0 copy-done.3
  6.9 0.0 copy-start.4
  6.9 0.8 %partial_latent.1 = (f32[64,256]{1,0:T(8,128)S(1)}, s32[4,128]{1,0:T(4,128)S(1)}, s32[4,128]{1,0:T(4,128)S(1)}) custom-call(s32[4]{0:T(128)S(1)} %copy-done.2, s32[4]{0:T(128)S(1)} %copy-done.3, bf16[256,1024]{1,0:T(8,128)(2,1)S(1)} %copy-done, bf16[4,64,1024]{2,1,0:T(8,128)(2,1)S(1)} %bitcast.19), custom_call_target="tpu_custom_call" | custom-call | flops 33554432 | bytes 655360 | tf_op jit(solution)/shard_map/partial_latent/pallas_call | solution.py:41
  7.7 0.1 collective-permute-start.3
  7.8 0.1 copy-done.4
  7.9 0.2 constant_dynamic-slice_fusion.4
  8.1 0.0 copy-start.6
  8.1 1.6 %collective-permute-start = (bf16[1024,128]{1,0:T(8,128)(2,1)S(1)}, bf16[1024,128]{1,0:T(8,128)(2,1)S(1)}, u32[]{:S(2)}, u32[]{:S(2)}) collective-permute-start(bf16[1024,128]{1,0:T(8,128)(2,1)S(1)} %bitcast.28), channel_id=1, source_target_pairs={{0,16},{16,0},{1,17},{17,1},{2,18},{18,2},{3,19},{19,3},{4,20},{20... | collective-permute-start | bytes 786440 | tf_op jit(solution)/shard_map/ppermute | solution.py:246
  9.7 0.0 collective-permute-done.3
  9.7 0.9 %collective-permute-start.4 = (f32[64,256]{1,0:T(8,128)S(1)}, f32[64,256]{1,0:T(8,128)S(1)}, u32[]{:S(2)}, u32[]{:S(2)}) collective-permute-start(f32[64,256]{1,0:T(8,128)S(1)} %add.24), channel_id=1, source_target_pairs={{0,16},{16,0},{1,17},{17,1},{2,18},{18,2},{3,19},{19,3},{4,20},{20... | collective-permute-start | bytes 196616 | tf_op jit(solution)/shard_map/ppermute | solution.py:207
  10.6 0.3 constant_dynamic-slice_fusion.2
  10.9 0.0 copy-start.8
  10.9 7.3 %collective-permute-done.4 = f32[64,256]{1,0:T(8,128)S(1)} collective-permute-done((f32[64,256]{1,0:T(8,128)S(1)}, f32[64,256]{1,0:T(8,128)S(1)}, u32[]{:S(2)}, u32[]{:S(2)}) %collective-permute-start.4) | collective-permute-done | bytes 65568 | tf_op jit(solution)/shard_map/ppermute | solution.py:207
  18.2 1.6 %collective-permute-start.5 = (f32[64,256]{1,0:T(8,128)S(1)}, f32[64,256]{1,0:T(8,128)S(1)}, u32[]{:S(2)}, u32[]{:S(2)}) collective-permute-start(f32[64,256]{1,0:T(8,128)S(1)} %add.25.first), channel_id=1, source_target_pairs={{0,2},{1,3},{2,0},{3,1},{4,6},{5,7},{6,4},{7,5},{8,10},{9,11},{10,... | collective-permute-start | bytes 196616 | tf_op jit(solution)/shard_map/ppermute | solution.py:207
  19.8 0.0 collective-permute-done.1.refs_2_
  19.8 0.5 %collective-permute-start.7 = (bf16[1024,128]{1,0:T(8,128)(2,1)S(1)}, bf16[1024,128]{1,0:T(8,128)(2,1)S(1)}, u32[]{:S(2)}, u32[]{:S(2)}) collective-permute-start(bf16[1024,128]{1,0:T(8,128)(2,1)S(1)} %collective-permute-done.1.refs_2_), channel_id=1, source_target_pairs={{0,4},{4,0},{8,12},{12,8},{1,5},{5,1},{9,13},{13,9},{2,6},{6,2},{1... | collective-permute-start | bytes 786440 | tf_op jit(solution)/shard_map/ppermute | solution.py:220
  20.2 0.0 copy-done.9
  20.2 0.3 constant_dynamic-slice_fusion
  20.6 1.9 %collective-permute-done.5.second = f32[64,256]{1,0:T(8,128)S(1)} collective-permute-done((f32[64,256]{1,0:T(8,128)S(1)}, f32[64,256]{1,0:T(8,128)S(1)}, u32[]{:S(2)}, u32[]{:S(2)}) %collective-permute-start.5) | collective-permute-done | bytes 65568 | tf_op jit(solution)/shard_map/ppermute | solution.py:207
  22.5 0.3 expand.1.refs_4_.refs_5_
  22.9 0.4 collective-permute-start.6
  23.3 0.7 %collective-permute-start.8 = (bf16[512,128]{1,0:T(8,128)(2,1)S(1)}, bf16[512,128]{1,0:T(8,128)(2,1)S(1)}, u32[]{:S(2)}, u32[]{:S(2)}) collective-permute-start(bf16[512,128]{1,0:T(8,128)(2,1)S(1)} %expand.1.refs_4_.refs_5_), channel_id=1, source_target_pairs={{0,4},{4,0},{8,12},{12,8},{1,5},{5,1},{9,13},{13,9},{2,6},{6,2},{1... | collective-permute-start | bytes 393224 | tf_op jit(solution)/shard_map/ppermute | solution.py:220
  23.9 0.0 collective-permute-done.2.refs_3_
  23.9 2.5 %attend.8 = (f32[1024,128]{1,0:T(8,128)S(1)}, f32[1024,256]{1,0:T(8,128)S(1)}) custom-call(bf16[1024,128]{1,0:T(8,128)(2,1)S(1)} %bitcast.20, bf16[1024,128]{1,0:T(8,128)(2,1)S(1)} %fusion.1.refs_1_, bf16[1024,128]{1,0:T(8,128)(2,1)S(1)} %collective-permute-done.1.refs_2_, bf16[1024,128]{1,0:T(8,128)(2,1)S(1)} %collective-permute-done.2.refs_3_), custom_call_target="tpu_custom_call" | custom-call | flops 1207959552 | bytes 524288 | tf_op jit(solution)/shard_map/attend/pallas_call | solution.py:184
  26.5 3.6 %collective-permute-done.6.refs_5_.refs_6_ = bf16[512,128]{1,0:T(8,128)(2,1)S(1)} collective-permute-done((bf16[512,128]{1,0:T(8,128)(2,1)S(1)}, bf16[512,128]{1,0:T(8,128)(2,1)S(1)}, u32[]{:S(2)}, u32[]{:S(2)}) %collective-permute-start.6) | collective-permute-done | bytes 131104 | tf_op jit(solution)/shard_map/ppermute | solution.py:220
  30.0 2.0 %collective-permute-start.9 = (bf16[512,128]{1,0:T(8,128)(2,1)S(1)}, bf16[512,128]{1,0:T(8,128)(2,1)S(1)}, u32[]{:S(2)}, u32[]{:S(2)}) collective-permute-start(bf16[512,128]{1,0:T(8,128)(2,1)S(1)} %collective-permute-done.6.refs_5_.refs_6_), channel_id=1, source_target_pairs={{0,4},{4,0},{8,12},{12,8},{1,5},{5,1},{9,13},{13,9},{2,6},{6,2},{1... | collective-permute-start | bytes 393224 | tf_op jit(solution)/shard_map/ppermute | solution.py:220
  32.0 0.0 collective-permute-done.refs_0_.refs_1_
  32.0 2.5 %attend.6 = (f32[1024,128]{1,0:T(8,128)S(1)}, f32[1024,256]{1,0:T(8,128)S(1)}) custom-call(bf16[1024,128]{1,0:T(8,128)(2,1)S(1)} %collective-permute-done.refs_0_.refs_1_, bf16[1024,128]{1,0:T(8,128)(2,1)S(1)} %fusion.1.refs_1_, bf16[1024,128]{1,0:T(8,128)(2,1)S(1)} %collective-permute-done.1.refs_2_, bf16[1024,128]{1,0:T(8,128)(2,1)S(1)} %collective-permute-done.2.refs_3_), custom_call_target="tpu_custom_call" | custom-call | flops 1207959552 | bytes 524288 | tf_op jit(solution)/shard_map/attend/pallas_call | solution.py:184
  34.5 0.0 collective-permute-done.7.refs_6_.refs_4_
  34.5 1.8 %attend.7 = (f32[1024,128]{1,0:T(8,128)S(1)}, f32[1024,256]{1,0:T(8,128)S(1)}) custom-call(s32[4,128]{1,0:T(4,128)S(1)} %get-tuple-element.23.refs_0_, bf16[1024,128]{1,0:T(8,128)(2,1)S(1)} %collective-permute-done.refs_0_.refs_1_, f32[1024,128]{1,0:T(8,128)S(1)} %get-tuple-element.24.refs_2_, f32[1024,256]{1,0:T(8,128)S(1)} %get-tuple-element.25.refs_3_, ...), custom_call_target="tpu_custom_call" | custom-call | flops 805306368 | bytes 524288 | tf_op jit(solution)/shard_map/attend/pallas_call | solution.py:184
  36.3 0.0 collective-permute-done.8.refs_7_.refs_4_
  36.4 0.7 %attend.10 = (f32[1024,128]{1,0:T(8,128)S(1)}, f32[1024,256]{1,0:T(8,128)S(1)}) custom-call(s32[4,128]{1,0:T(4,128)S(1)} %get-tuple-element.23.refs_0_, bf16[1024,128]{1,0:T(8,128)(2,1)S(1)} %collective-permute-done.refs_0_.refs_1_, f32[1024,128]{1,0:T(8,128)S(1)} %get-tuple-element.37.refs_2_, f32[1024,256]{1,0:T(8,128)S(1)} %get-tuple-element.38.refs_3_, ...), custom_call_target="tpu_custom_call" | custom-call | flops 201326592 | bytes 524288 | tf_op jit(solution)/shard_map/attend/pallas_call | solution.py:184
  37.1 0.0 collective-permute-done.9.refs_8_.refs_4_
  37.1 0.7 %attend.11 = bf16[1024,128]{1,0:T(8,128)(2,1)S(1)} custom-call(s32[4,128]{1,0:T(4,128)S(1)} %get-tuple-element.23.refs_0_, bf16[1024,128]{1,0:T(8,128)(2,1)S(1)} %collective-permute-done.refs_0_.refs_1_, f32[1024,128]{1,0:T(8,128)S(1)} %get-tuple-element.39.refs_2_, f32[1024,256]{1,0:T(8,128)S(1)} %get-tuple-element.40.refs_3_, ...), custom_call_target="tpu_custom_call" | custom-call | flops 201326592 | bytes 524288 | tf_op jit(solution)/shard_map/attend/pallas_call | solution.py:184
  37.8 1.6 %collective-permute-start.10 = (bf16[1024,128]{1,0:T(8,128)(2,1)S(1)}, bf16[1024,128]{1,0:T(8,128)(2,1)S(1)}, u32[]{:S(2)}, u32[]{:S(2)}) collective-permute-start(bf16[1024,128]{1,0:T(8,128)(2,1)S(1)} %attend.11), channel_id=1, source_target_pairs={{0,16},{16,0},{1,17},{17,1},{2,18},{18,2},{3,19},{19,3},{4,20},{20... | collective-permute-start | bytes 786440 | tf_op jit(solution)/shard_map/ppermute | solution.py:246
  39.4 2.7 %attend.9 = bf16[1024,128]{1,0:T(8,128)(2,1)S(1)} custom-call(s32[4,128]{1,0:T(4,128)S(1)} %get-tuple-element.23.refs_0_, bf16[1024,128]{1,0:T(8,128)(2,1)S(1)} %bitcast.21, f32[1024,128]{1,0:T(8,128)S(1)} %get-tuple-element.34.refs_2_, f32[1024,256]{1,0:T(8,128)S(1)} %get-tuple-element.35.refs_3_, ...), custom_call_target="tpu_custom_call" | custom-call | flops 1207959552 | bytes 524288 | tf_op jit(solution)/shard_map/attend/pallas_call | solution.py:184
  42.1 0.7 %place.2.refs_0_ = bf16[256,2,4,128]{3,2,1,0:T(4,128)(2,1)} custom-call(bf16[256,4,128]{2,1,0:T(4,128)(2,1)S(1)} %bitcast.23), custom_call_target="tpu_custom_call" | custom-call | tf_op jit(solution)/shard_map/place/pallas_call | solution.py:106
  42.8 1.4 %collective-permute-done.10 = bf16[1024,128]{1,0:T(8,128)(2,1)S(1)} collective-permute-done((bf16[1024,128]{1,0:T(8,128)(2,1)S(1)}, bf16[1024,128]{1,0:T(8,128)(2,1)S(1)}, u32[]{:S(2)}, u32[]{:S(2)}) %collective-permute-start.10) | collective-permute-done | bytes 262176 | tf_op jit(solution)/shard_map/ppermute | solution.py:246
  44.3 0.7 %place.3 = bf16[256,2,4,128]{3,2,1,0:T(4,128)(2,1)} custom-call(bf16[256,2,4,128]{3,2,1,0:T(4,128)(2,1)} %place.2.refs_0_, bf16[256,4,128]{2,1,0:T(4,128)(2,1)S(1)} %bitcast.22), custom_call_target="tpu_custom_call", output_to_operand_aliasing={{}: (0, {})} | custom-call | tf_op jit(solution)/shard_map/place/pallas_call | solution.py:106
  (16 shorter events, 0.1 us)
Async XLA Ops:
  0.0 1.0 %copy-start.5 = (bf16[512,2,128]{2,1,0:T(2,128)(2,1)S(1)}, bf16[512,2,128]{2,1,0:T(2,128)(2,1)}, u32[]{:S(2)}) copy-start(bf16[512,2,128]{2,1,0:T(2,128)(2,1)} %param.19) | copy-start | bytes 786436
  1.0 5.8 %copy-start.1 = (bf16[4,1024,64]{1,2,0:T(8,128)(2,1)S(1)}, bf16[4,1024,64]{1,2,0:T(8,128)(2,1)}, u32[]{:S(2)}) copy-start(bf16[4,1024,64]{1,2,0:T(8,128)(2,1)} %param.13) | copy-start | bytes 1572868
  1.1 5.8 %copy-start = (bf16[256,1024]{1,0:T(8,128)(2,1)S(1)}, bf16[256,1024]{1,0:T(8,128)(2,1)}, u32[]{:S(2)}) copy-start(bf16[256,1024]{1,0:T(8,128)(2,1)} %features_ref.1) | copy-start | bytes 1572868
  1.1 5.7 %copy-start.2 = (s32[4]{0:T(128)S(1)}, s32[4]{0:T(128)}, u32[]{:S(2)}) copy-start(s32[4]{0:T(128)} %ids_ref.1) | copy-start | bytes 52
  1.2 5.7 %copy-start.3 = (s32[4]{0:T(128)S(1)}, s32[4]{0:T(128)}, u32[]{:S(2)}) copy-start(s32[4]{0:T(128)} %order_ref.1) | copy-start | bytes 52
  1.2 18.6 %collective-permute-start.1 = (bf16[1024,128]{1,0:T(8,128)(2,1)S(1)}, bf16[1024,128]{1,0:T(8,128)(2,1)S(1)}, u32[]{:S(2)}, u32[]{:S(2)}) collective-permute-start(bf16[1024,128]{1,0:T(8,128)(2,1)S(1)} %fusion.1.refs_1_), channel_id=1, source_target_pairs={{0,8},{4,12},{8,0},{12,4},{1,9},{5,13},{9,1},{13,5},{2,10},{6,14},... | collective-permute-start | bytes 786440 | tf_op jit(solution)/shard_map/ppermute | solution.py:220
  5.3 18.6 %collective-permute-start.2 = (bf16[1024,128]{1,0:T(8,128)(2,1)S(1)}, bf16[1024,128]{1,0:T(8,128)(2,1)S(1)}, u32[]{:S(2)}, u32[]{:S(2)}) collective-permute-start(bf16[1024,128]{1,0:T(8,128)(2,1)S(1)} %fusion.1.refs_1_), channel_id=1, source_target_pairs={{0,4},{4,0},{8,12},{12,8},{1,5},{5,1},{9,13},{13,9},{2,6},{6,2},{1... | collective-permute-start | bytes 786440 | tf_op jit(solution)/shard_map/ppermute | solution.py:220
  6.9 1.0 %copy-start.4 = (bf16[256,2,4,128]{3,2,1,0:T(4,128)(2,1)S(1)}, bf16[256,2,4,128]{3,2,1,0:T(4,128)(2,1)}, u32[]{:S(2)}) copy-start(bf16[256,2,4,128]{3,2,1,0:T(4,128)(2,1)} %param.11) | copy-start | bytes 1572868
  7.7 2.0 %collective-permute-start.3 = (f32[64,256]{1,0:T(8,128)S(1)}, f32[64,256]{1,0:T(8,128)S(1)}, u32[]{:S(2)}, u32[]{:S(2)}) collective-permute-start(f32[64,256]{1,0:T(8,128)S(1)} %get-tuple-element.27), channel_id=1, source_target_pairs={{0,1},{1,0},{2,3},{3,2},{4,5},{5,4},{6,7},{7,6},{8,9},{9,8},{10,11... | collective-permute-start | bytes 196616 | tf_op jit(solution)/shard_map/ppermute | solution.py:207
  7.9 2.7 %copy-start.7 = (bf16[4,64,2,128]{3,2,1,0:T(2,128)(2,1)S(1)}, bf16[4,64,2,128]{3,2,1,0:T(2,128)(2,1)}, u32[]{:S(2)}) copy-start(bf16[4,64,2,128]{3,2,1,0:T(2,128)(2,1)} %param.14) | copy-start | bytes 393220
  8.1 2.5 %copy-start.6 = (bf16[4,64,2,128]{3,2,1,0:T(2,128)(2,1)S(1)}, bf16[4,64,2,128]{3,2,1,0:T(2,128)(2,1)}, u32[]{:S(2)}) copy-start(bf16[4,64,2,128]{3,2,1,0:T(2,128)(2,1)} %param.15) | copy-start | bytes 393220
  8.1 23.9 %collective-permute-start = (bf16[1024,128]{1,0:T(8,128)(2,1)S(1)}, bf16[1024,128]{1,0:T(8,128)(2,1)S(1)}, u32[]{:S(2)}, u32[]{:S(2)}) collective-permute-start(bf16[1024,128]{1,0:T(8,128)(2,1)S(1)} %bitcast.28), channel_id=1, source_target_pairs={{0,16},{16,0},{1,17},{17,1},{2,18},{18,2},{3,19},{19,3},{4,20},{20... | collective-permute-start | bytes 786440 | tf_op jit(solution)/shard_map/ppermute | solution.py:246
  9.7 8.5 %collective-permute-start.4 = (f32[64,256]{1,0:T(8,128)S(1)}, f32[64,256]{1,0:T(8,128)S(1)}, u32[]{:S(2)}, u32[]{:S(2)}) collective-permute-start(f32[64,256]{1,0:T(8,128)S(1)} %add.24), channel_id=1, source_target_pairs={{0,16},{16,0},{1,17},{17,1},{2,18},{18,2},{3,19},{19,3},{4,20},{20... | collective-permute-start | bytes 196616 | tf_op jit(solution)/shard_map/ppermute | solution.py:207
  10.6 9.6 %copy-start.9 = (bf16[256,2,128]{2,1,0:T(2,128)(2,1)S(1)}, bf16[256,2,128]{2,1,0:T(2,128)(2,1)}, u32[]{:S(2)}) copy-start(bf16[256,2,128]{2,1,0:T(2,128)(2,1)} %param.16) | copy-start | bytes 393220
  10.9 9.3 %copy-start.8 = (bf16[256,2,128]{2,1,0:T(2,128)(2,1)S(1)}, bf16[256,2,128]{2,1,0:T(2,128)(2,1)}, u32[]{:S(2)}) copy-start(bf16[256,2,128]{2,1,0:T(2,128)(2,1)} %param.17) | copy-start | bytes 393220
  18.2 4.3 %collective-permute-start.5 = (f32[64,256]{1,0:T(8,128)S(1)}, f32[64,256]{1,0:T(8,128)S(1)}, u32[]{:S(2)}, u32[]{:S(2)}) collective-permute-start(f32[64,256]{1,0:T(8,128)S(1)} %add.25.first), channel_id=1, source_target_pairs={{0,2},{1,3},{2,0},{3,1},{4,6},{5,7},{6,4},{7,5},{8,10},{9,11},{10,... | collective-permute-start | bytes 196616 | tf_op jit(solution)/shard_map/ppermute | solution.py:207
  19.8 14.7 %collective-permute-start.7 = (bf16[1024,128]{1,0:T(8,128)(2,1)S(1)}, bf16[1024,128]{1,0:T(8,128)(2,1)S(1)}, u32[]{:S(2)}, u32[]{:S(2)}) collective-permute-start(bf16[1024,128]{1,0:T(8,128)(2,1)S(1)} %collective-permute-done.1.refs_2_), channel_id=1, source_target_pairs={{0,4},{4,0},{8,12},{12,8},{1,5},{5,1},{9,13},{13,9},{2,6},{6,2},{1... | collective-permute-start | bytes 786440 | tf_op jit(solution)/shard_map/ppermute | solution.py:220
  22.9 7.2 %collective-permute-start.6 = (bf16[512,128]{1,0:T(8,128)(2,1)S(1)}, bf16[512,128]{1,0:T(8,128)(2,1)S(1)}, u32[]{:S(2)}, u32[]{:S(2)}) collective-permute-start(bf16[512,128]{1,0:T(8,128)(2,1)S(1)} %expand.1.refs_4_.refs_5_), channel_id=1, source_target_pairs={{0,8},{4,12},{8,0},{12,4},{1,9},{5,13},{9,1},{13,5},{2,10},{6,14},... | collective-permute-start | bytes 393224 | tf_op jit(solution)/shard_map/ppermute | solution.py:220
  23.3 13.1 %collective-permute-start.8 = (bf16[512,128]{1,0:T(8,128)(2,1)S(1)}, bf16[512,128]{1,0:T(8,128)(2,1)S(1)}, u32[]{:S(2)}, u32[]{:S(2)}) collective-permute-start(bf16[512,128]{1,0:T(8,128)(2,1)S(1)} %expand.1.refs_4_.refs_5_), channel_id=1, source_target_pairs={{0,4},{4,0},{8,12},{12,8},{1,5},{5,1},{9,13},{13,9},{2,6},{6,2},{1... | collective-permute-start | bytes 393224 | tf_op jit(solution)/shard_map/ppermute | solution.py:220
  30.0 7.1 %collective-permute-start.9 = (bf16[512,128]{1,0:T(8,128)(2,1)S(1)}, bf16[512,128]{1,0:T(8,128)(2,1)S(1)}, u32[]{:S(2)}, u32[]{:S(2)}) collective-permute-start(bf16[512,128]{1,0:T(8,128)(2,1)S(1)} %collective-permute-done.6.refs_5_.refs_6_), channel_id=1, source_target_pairs={{0,4},{4,0},{8,12},{12,8},{1,5},{5,1},{9,13},{13,9},{2,6},{6,2},{1... | collective-permute-start | bytes 393224 | tf_op jit(solution)/shard_map/ppermute | solution.py:220
  37.8 6.4 %collective-permute-start.10 = (bf16[1024,128]{1,0:T(8,128)(2,1)S(1)}, bf16[1024,128]{1,0:T(8,128)(2,1)S(1)}, u32[]{:S(2)}, u32[]{:S(2)}) collective-permute-start(bf16[1024,128]{1,0:T(8,128)(2,1)S(1)} %attend.11), channel_id=1, source_target_pairs={{0,16},{16,0},{1,17},{17,1},{2,18},{18,2},{3,19},{19,3},{4,20},{20... | collective-permute-start | bytes 786440 | tf_op jit(solution)/shard_map/ppermute | solution.py:246
